TPU v7x, 32 devices: a whole 2x2x4 slice. The times are simulated.
32 devices in a mesh: dp: 8 (over y, x, core), tensor: 4 (over z).
Axes of the slice: x: 2, y: 2, z: 4, core: 2. Of those that a mesh axis runs over, the one named last changes fastest.
Arguments:
- layer_input: bfloat16 [32768, 768], P('dp'), may hold values from -6 to 6
- segments: int32 [32, 1024], P('dp'), may hold values from 0 to 7, never falling along the last dimension, each value on 1 to 512 neighbouring positions
- query_weight: bfloat16 [768, 768], P(None, 'tensor'), may hold values from -0.21875 to 0.21875
- query_bias: float32 [768], P('tensor'), may hold values from -3 to 3
- key_weight: bfloat16 [768, 768], P(None, 'tensor'), may hold values from -0.21875 to 0.21875
- value_weight: bfloat16 [768, 768], P(None, 'tensor'), may hold values from -0.21875 to 0.21875
- value_bias: float32 [768], P('tensor'), may hold values from -3 to 3
- output_weight: bfloat16 [768, 768], P('tensor'), may hold values from -0.875 to 0.875
- output_bias: float32 [768], replicated, may hold values from -3 to 3
- first_gain: float32 [768], replicated, may hold values from 0.5 to 1.5
- first_shift: float32 [768], replicated, may hold values from -3 to 3
- up_weight: bfloat16 [768, 3072], P(None, 'tensor'), may hold values from -0.21875 to 0.21875
- up_bias: float32 [3072], P('tensor'), may hold values from -3 to 3
- down_weight: bfloat16 [3072, 768], P('tensor'), may hold values from -0.109375 to 0.109375
- down_bias: float32 [768], replicated, may hold values from -3 to 3
- second_gain: float32 [768], replicated, may hold values from 0.5 to 1.5
- second_shift: float32 [768], replicated, may hold values from -3 to 3
- output_grad: bfloat16 [32768, 768], P('dp'), may hold values from -6 to 6
Outputs:
- layer_output: bfloat16 [32768, 768], P(('dp', 'tensor'))
- input_grad: float32 [32768, 768], P(('dp', 'tensor'))
- grad_query_weight: float32 [768, 768], P('dp', 'tensor')
- grad_query_bias: float32 [768], P('tensor')
- grad_key_weight: float32 [768, 768], P('dp', 'tensor')
- grad_value_weight: float32 [768, 768], P('dp', 'tensor')
- grad_value_bias: float32 [768], P('tensor')
- grad_output_weight: float32 [768, 768], P('tensor', 'dp')
- grad_output_bias: float32 [768], P(('dp', 'tensor'))
- grad_first_gain: float32 [768], P(('dp', 'tensor'))
- grad_first_shift: float32 [768], P(('dp', 'tensor'))
- grad_up_weight: float32 [768, 3072], P('dp', 'tensor')
- grad_up_bias: float32 [3072], P('tensor')
- grad_down_weight: float32 [3072, 768], P('tensor', 'dp')
- grad_down_bias: float32 [768], P(('dp', 'tensor'))
- grad_second_gain: float32 [768], P(('dp', 'tensor'))
- grad_second_shift: float32 [768], P(('dp', 'tensor'))
Inputs may be any that keep to these rules, and one draw needn't show every extreme that they name: `segments`: segment numbers restart in every packed row; a token attends exactly to the tokens of its own row that carry its segment number.
All inputs are finite; a program needn't handle non-finite values.
Results may differ from a plain program's by a relative error of at most 0.02.
The roundings to bfloat16 on the way count: a program that leaves them out, or rounds other values in their place, can miss the bound.
Values may be sent and summed in bfloat16 or wider, within the bound.
A program may use at most 256 MiB of HBM per device.

v0:
```python
import functools

import jax
import jax.numpy as jnp
from jax import lax
from jax.experimental import pallas as pl
from jax.experimental.pallas import tpu as pltpu
from jax.sharding import PartitionSpec as P

HEAD_DIM = 64
GROUP_HEADS = 3

norm_eps = 1e-06


def product(left_side, right_side):
    return jnp.dot(left_side, right_side, preferred_element_type=jnp.float32)


def contract_rows(left_side, right_side):
    return lax.dot_general(
        left_side, right_side, (((0,), (0,)), ((), ())), preferred_element_type=jnp.float32
    )


def contract_last(left_side, right_side):
    return lax.dot_general(
        left_side, right_side, (((1,), (1,)), ((), ())), preferred_element_type=jnp.float32
    )


def normalize(summed, norm_gain, offset):
    centred = summed - jnp.mean(summed, -1, keepdims=True)
    inverse = lax.rsqrt(jnp.mean(centred * centred, -1, keepdims=True) + norm_eps)
    scaled = centred * inverse
    return (scaled * norm_gain + offset, scaled, inverse)


def normalize_back(grad_out, scaled, inverse, norm_gain):
    grad_scaled = grad_out * norm_gain
    mean_grad = jnp.mean(grad_scaled, -1, keepdims=True)
    mean_cross = jnp.mean(grad_scaled * scaled, -1, keepdims=True)
    return inverse * (grad_scaled - mean_grad - scaled * mean_cross)


def gelu_tanh(pre_act):
    return jax.nn.gelu(pre_act, approximate=True)


SCALE = HEAD_DIM ** (-0.5)
STATS = 128


def _scores(q, k, linked):
    s = lax.dot_general(q, k, (((1,), (1,)), ((), ())), preferred_element_type=jnp.float32) * SCALE
    return jnp.where(linked, s, -1e30)


def attn_fwd_kernel(q_ref, k_ref, v_ref, segq_ref, segk_ref, ctx_ref, stats_ref):
    linked = segq_ref[...] == segk_ref[...]
    heads = q_ref.shape[1] // HEAD_DIM
    half = STATS // 2
    for h in range(heads):
        cols = slice(h * HEAD_DIM, (h + 1) * HEAD_DIM)
        s = _scores(q_ref[:, cols], k_ref[:, cols], linked)
        m = jnp.max(s, axis=1, keepdims=True)
        e = jnp.exp(s - m)
        l = jnp.sum(e, axis=1, keepdims=True)
        p = (e / l).astype(jnp.bfloat16)
        ctx = jnp.dot(p, v_ref[:, cols], preferred_element_type=jnp.float32)
        ctx_ref[:, cols] = ctx.astype(ctx_ref.dtype)
        stats_ref[:, h : h + 1] = m
        stats_ref[:, half + h : half + h + 1] = l


def attn_bwd_kernel(parts, q_ref, k_ref, v_ref, dctx_ref, segq_ref, segk_ref, stats_ref, x_ref, xall_ref,
                    out_t_ref, dq_ref, dk_ref, dv_ref, wgrad_ref, bias_ref, dk_acc, dv_acc, dwq_acc):
    step = pl.program_id(0)

    @pl.when(step == 0)
    def _():
        dk_acc[...] = jnp.zeros_like(dk_acc)
        dv_acc[...] = jnp.zeros_like(dv_acc)
        dwq_acc[...] = jnp.zeros_like(dwq_acc)
        bias_ref[...] = jnp.zeros_like(bias_ref)

    linked = segq_ref[...] == segk_ref[...]
    heads = q_ref.shape[1] // HEAD_DIM
    half = STATS // 2
    dq_parts = []
    for h in range(heads):
        cols = slice(h * HEAD_DIM, (h + 1) * HEAD_DIM)
        q = q_ref[:, cols]
        k = k_ref[:, cols]
        dctx = dctx_ref[:, cols]
        s = _scores(q, k, linked)
        p = jnp.exp(s - stats_ref[:, h : h + 1]) / stats_ref[:, half + h : half + h + 1]
        dp = lax.dot_general(dctx, v_ref[:, cols], (((1,), (1,)), ((), ())), preferred_element_type=jnp.float32)
        inner = jnp.sum(p * dp, axis=1, keepdims=True)
        ds = (p * (dp - inner)).astype(jnp.bfloat16)
        dq = (jnp.dot(ds, k, preferred_element_type=jnp.float32) * SCALE).astype(dq_ref.dtype)
        dq_ref[:, cols] = dq
        dq_parts.append(dq)
        dk_acc[:, cols] += lax.dot_general(ds, q, (((0,), (0,)), ((), ())), preferred_element_type=jnp.float32)
        dv_acc[:, cols] += lax.dot_general(p.astype(jnp.bfloat16), dctx, (((0,), (0,)), ((), ())), preferred_element_type=jnp.float32)
    dq_block = jnp.concatenate(dq_parts, axis=1)
    dwq_acc[...] += lax.dot_general(x_ref[...], dq_block, (((0,), (0,)), ((), ())), preferred_element_type=jnp.float32)
    bias_ref[0:1, :] += jnp.sum(dq_block.astype(jnp.float32), axis=0, keepdims=True)

    @pl.when(step == pl.num_programs(0) - 1)
    def _():
        width = dk_ref.shape[1]
        dk = (dk_acc[...] * SCALE).astype(dk_ref.dtype)
        dv = dv_acc[...].astype(dv_ref.dtype)
        dk_ref[...] = dk
        dv_ref[...] = dv
        bias_ref[1:2, :] = jnp.sum(dv.astype(jnp.float32), axis=0, keepdims=True)
        xall = xall_ref[...]
        grads = (
            dwq_acc[...].astype(wgrad_ref.dtype),
            lax.dot_general(xall, dk, (((0,), (0,)), ((), ())),
                            preferred_element_type=jnp.float32).astype(wgrad_ref.dtype),
            lax.dot_general(xall, dv, (((0,), (0,)), ((), ())),
                            preferred_element_type=jnp.float32).astype(wgrad_ref.dtype),
            out_t_ref[...],
        )
        piece = width // parts
        for part in range(parts):
            for index, grad in enumerate(grads):
                start = (part * len(grads) + index) * piece
                wgrad_ref[:, start : start + piece] = grad[:, part * piece : (part + 1) * piece]


def attention_forward(queries, key_side, value_proj, segment_row, block=256):
    length, width = queries.shape
    segq = segment_row.reshape(length, 1)
    segk = segment_row.reshape(1, length)
    full = pl.BlockSpec((length, width), lambda i: (0, 0))
    return pl.pallas_call(
        attn_fwd_kernel,
        out_shape=(jax.ShapeDtypeStruct((length, width), jnp.bfloat16),
                   jax.ShapeDtypeStruct((length, STATS), jnp.float32)),
        grid=(length // block,),
        in_specs=[pl.BlockSpec((block, width), lambda i: (i, 0)), full, full,
                  pl.BlockSpec((block, 1), lambda i: (i, 0)),
                  pl.BlockSpec((1, length), lambda i: (0, 0))],
        out_specs=(pl.BlockSpec((block, width), lambda i: (i, 0)),
                   pl.BlockSpec((block, STATS), lambda i: (i, 0))),
        compiler_params=pltpu.CompilerParams(dimension_semantics=("arbitrary",)),
        cost_estimate=pl.CostEstimate(flops=4 * length * length * width, transcendentals=length * length * width // HEAD_DIM,
                                      bytes_accessed=8 * length * width),
    )(queries, key_side, value_proj, segq, segk)


def attention_backward(queries, key_side, value_proj, segment_row, stats, grad_context, inputs, out_t, parts,
                       block=256):
    length, width = queries.shape
    features = inputs.shape[1]
    segq = segment_row.reshape(length, 1)
    segk = segment_row.reshape(1, length)
    full = pl.BlockSpec((length, width), lambda i: (0, 0))
    rows = pl.BlockSpec((block, width), lambda i: (i, 0))
    return pl.pallas_call(
        functools.partial(attn_bwd_kernel, parts),
        out_shape=tuple(jax.ShapeDtypeStruct((length, width), jnp.bfloat16) for _ in range(3))
        + (jax.ShapeDtypeStruct((features, 4 * width), jnp.bfloat16),
           jax.ShapeDtypeStruct((8, width), jnp.float32)),
        grid=(length // block,),
        in_specs=[rows, full, full, rows,
                  pl.BlockSpec((block, 1), lambda i: (i, 0)),
                  pl.BlockSpec((1, length), lambda i: (0, 0)),
                  pl.BlockSpec((block, STATS), lambda i: (i, 0)),
                  pl.BlockSpec((block, features), lambda i: (i, 0)),
                  pl.BlockSpec((length, features), lambda i: (0, 0)),
                  pl.BlockSpec((features, width), lambda i: (0, 0))],
        out_specs=(rows, full, full,
                   pl.BlockSpec((features, 4 * width), lambda i: (0, 0)),
                   pl.BlockSpec((8, width), lambda i: (0, 0))),
        scratch_shapes=[pltpu.VMEM((length, width), jnp.float32), pltpu.VMEM((length, width), jnp.float32),
                        pltpu.VMEM((features, width), jnp.float32)],
        compiler_params=pltpu.CompilerParams(dimension_semantics=("arbitrary",), vmem_limit_bytes=60 * 1024 * 1024),
        cost_estimate=pl.CostEstimate(flops=10 * length * length * width + 6 * length * features * width,
                                      transcendentals=length * length * width // HEAD_DIM,
                                      bytes_accessed=14 * length * width + 10 * features * width),
    )(queries, key_side, value_proj, grad_context, segq, segk, stats, inputs, inputs, out_t)


def gather_shards(first_pieces, second_pieces, after=None):
    dp_count = lax.axis_size("dp")
    core = lax.rem(lax.axis_index("dp"), 2)
    first, second = jnp.stack(first_pieces), jnp.stack(second_pieces)
    mine = jnp.where(core == 0, first, second)
    gathered = lax.all_gather(mine, "tensor", axis=0, tiled=False)
    if after is not None:
        gathered, after = lax.optimization_barrier((gathered, after))
    other = lax.ppermute(gathered, "dp", perm=[(i, i ^ 1) for i in range(dp_count)])
    halves = (jnp.where(core == 0, gathered, other), jnp.where(core == 0, other, gathered))
    return [half[:, index] for half in halves for index in range(half.shape[1])]


def gather_pieces(pieces, after):
    dp_count = lax.axis_size("dp")
    part_count = lax.axis_size("tensor")
    rows = pieces[0].shape[0] // dp_count
    own = lax.dynamic_slice_in_dim(jnp.stack(pieces), lax.axis_index("dp") * rows, rows, 1)
    gathered = lax.all_gather(own, ("dp", "tensor"), axis=0, tiled=False)
    gathered, after = lax.optimization_barrier((gathered, after))
    gathered = gathered.reshape((dp_count, part_count) + own.shape)
    stacks = gathered.transpose(2, 1, 0, 3, 4).reshape(
        (len(pieces), part_count, dp_count * rows) + own.shape[2:]
    )
    return [stacks[index] for index in range(len(pieces))]


def scatter_rows(grads):
    joined = jnp.concatenate([grad.astype(jnp.bfloat16) for grad in grads], axis=1)
    return lax.psum_scatter(joined, "dp", scatter_dimension=0, tiled=True)


def part_major(grads):
    parts = lax.axis_size("tensor")
    columns = []
    for part in range(parts):
        for grad in grads:
            width = grad.shape[1] // parts
            columns.append(grad[:, part * width : (part + 1) * width].astype(jnp.bfloat16))
    return jnp.concatenate(columns, axis=1)


def scatter_parts(partials, widths):
    parts = lax.axis_size("tensor")
    joined = jnp.concatenate(
        [partial.reshape(partial.shape[0], parts, -1) for partial in partials], axis=2
    )
    summed = lax.psum_scatter(joined, "tensor", scatter_dimension=1, tiled=True)[:, 0]
    pieces = []
    start = 0
    for group in widths:
        for width in group:
            pieces.append(summed[:, start : start + width].astype(jnp.float32))
            start += width
    return pieces


def on_device(
    layer_input,
    segments,
    query_weight,
    query_bias,
    key_weight,
    value_weight,
    value_bias,
    output_weight,
    output_bias,
    first_gain,
    first_shift,
    up_weight,
    up_bias,
    down_weight,
    down_bias,
    second_gain,
    second_shift,
    output_grad,
):
    part_count = lax.axis_size("tensor")
    part_id = lax.axis_index("tensor")
    row_len = segments.shape[1]

    input_rows = lax.dynamic_slice_in_dim(layer_input, part_id * row_len, row_len, 0)
    segment_row = lax.dynamic_index_in_dim(segments, part_id, 0, keepdims=False)
    grad_out = lax.dynamic_slice_in_dim(output_grad, part_id * row_len, row_len, 0).astype(
        jnp.float32
    )

    qt_sh, kt_sh, vt_sh, o_sh = gather_shards(
        [query_weight.T, key_weight.T], [value_weight.T, output_weight]
    )
    bias_sh = lax.all_gather(
        jnp.concatenate([query_bias, value_bias, up_bias]), "tensor", axis=0, tiled=False
    )
    head_width = query_bias.shape[0]
    qb = bias_sh[:, :head_width].reshape(-1)
    vb = bias_sh[:, head_width : 2 * head_width].reshape(-1)
    ub = bias_sh[:, 2 * head_width :]
    width = qt_sh.shape[2]
    qt_full = qt_sh.reshape(-1, width)
    kt_full = kt_sh.reshape(-1, width)
    vt_full = vt_sh.reshape(-1, width)

    input_f32 = input_rows.astype(jnp.float32)
    queries = (contract_last(input_rows, qt_full) + qb).astype(jnp.bfloat16)
    key_side = contract_last(input_rows, kt_full).astype(jnp.bfloat16)
    value_proj = (contract_last(input_rows, vt_full) + vb).astype(jnp.bfloat16)
    context, softmax_stats = attention_forward(queries, key_side, value_proj, segment_row)
    u_sh, d_sh = gather_pieces([up_weight, down_weight], context)

    group_width = o_sh.shape[1]
    attn_total = input_f32
    for member in range(part_count):
        cols = slice(member * group_width, (member + 1) * group_width)
        attn_total = attn_total + product(context[:, cols], o_sh[member]).astype(
            jnp.bfloat16
        ).astype(jnp.float32)
    first_in = attn_total + output_bias
    first_out, first_unit, first_inv = normalize(first_in, first_gain, first_shift)
    first_low = first_out.astype(jnp.bfloat16)
    second_in = first_out
    pulls = []
    hidden_parts = []
    for member in range(part_count):
        pre_part = product(first_low, u_sh[member]) + ub[member]
        gelu_out, pull_gelu = jax.vjp(gelu_tanh, pre_part)
        pulls.append(pull_gelu)
        hidden_part = gelu_out.astype(jnp.bfloat16)
        hidden_parts.append(hidden_part)
        second_in = second_in + product(hidden_part, d_sh[member]).astype(
            jnp.bfloat16
        ).astype(jnp.float32)
    second_in = second_in + down_bias
    second_out, second_unit, second_inv = normalize(second_in, second_gain, second_shift)
    layer_output = second_out.astype(jnp.bfloat16)

    grad_second = normalize_back(grad_out, second_unit, second_inv, second_gain)
    grad_second_gain = jnp.sum(grad_out * second_unit, 0)
    grad_second_shift = jnp.sum(grad_out, 0)
    grad_down_bias = jnp.sum(grad_second, 0)
    down_low = grad_second.astype(jnp.bfloat16)
    first_grad = grad_second
    grad_pre_parts = []
    for member in range(part_count):
        grad_hidden = contract_last(down_low, d_sh[member])
        grad_pre = pulls[member](grad_hidden)[0].astype(jnp.bfloat16)
        grad_pre_parts.append(grad_pre)
        first_grad = first_grad + contract_last(grad_pre, u_sh[member])
    grad_pre = jnp.concatenate(grad_pre_parts, axis=1)
    hidden_low = jnp.concatenate(hidden_parts, axis=1)
    grad_up_bias = jnp.sum(grad_pre, 0, dtype=jnp.float32)
    ffn_grads = [contract_rows(first_low, grad_pre), contract_rows(down_low, hidden_low)]
    ffn_joined, first_grad = lax.optimization_barrier((part_major(ffn_grads), first_grad))
    ffn_rows = scatter_rows([ffn_joined])
    grad_first_gain = jnp.sum(first_grad * first_unit, 0)
    grad_first_shift = jnp.sum(first_grad, 0)
    attn_grad = normalize_back(first_grad, first_unit, first_inv, first_gain)
    grad_output_bias = jnp.sum(attn_grad, 0)
    attn_grad_low = attn_grad.astype(jnp.bfloat16)
    grad_context = contract_last(attn_grad_low, o_sh.reshape(-1, o_sh.shape[2])).astype(
        jnp.bfloat16
    )
    output_grad_t = contract_rows(attn_grad_low, context).astype(jnp.bfloat16)
    query_low, key_low, value_low, attn_joined, qv_bias = attention_backward(
        queries, key_side, value_proj, segment_row, softmax_stats, grad_context, input_rows,
        output_grad_t, part_count,
    )
    ffn_rows, attn_joined, qv_bias = lax.optimization_barrier((ffn_rows, attn_joined, qv_bias))
    grad_query_bias = qv_bias[0]
    grad_value_bias = qv_bias[1]
    attn_rows = scatter_rows([attn_joined])
    small = lax.psum(
        jnp.concatenate(
            [
                grad_query_bias,
                grad_value_bias,
                grad_up_bias,
                grad_output_bias,
                grad_first_gain,
                grad_first_shift,
                grad_down_bias,
                grad_second_gain,
                grad_second_shift,
            ]
        ),
        ("dp", "tensor"),
    )
    input_grad = (
        attn_grad
        + product(query_low, qt_full)
        + product(key_low, kt_full)
        + product(value_low, vt_full)
    )
    attn_rows, small, input_grad = lax.optimization_barrier((attn_rows, small, input_grad))
    ffn_width = up_weight.shape[1]
    summed = scatter_parts([ffn_rows, attn_rows], [[ffn_width] * 2, [head_width] * 4])
    split_width = 2 * head_width * part_count + up_bias.shape[0] * part_count
    split = small[:split_width]
    shared = small[split_width:].reshape(6, -1)
    device_id = lax.axis_index("dp") * part_count + part_id
    piece = shared.shape[1] // (lax.axis_size("dp") * part_count)
    shared = lax.dynamic_slice_in_dim(shared, device_id * piece, piece, 1)

    def own_block(vector, offset, width):
        return lax.dynamic_slice_in_dim(vector, offset + part_id * width, width, 0)

    query_bias_grad = own_block(split, 0, head_width)
    value_bias_grad = own_block(split, head_width * part_count, head_width)
    up_bias_grad = own_block(split, 2 * head_width * part_count, up_bias.shape[0])
    return (
        layer_output,
        input_grad,
        summed[2],
        query_bias_grad,
        summed[3],
        summed[4],
        value_bias_grad,
        summed[5].T,
        shared[0],
        shared[1],
        shared[2],
        summed[0],
        up_bias_grad,
        summed[1].T,
        shared[3],
        shared[4],
        shared[5],
    )


def solution(mesh):
    in_specs = (
        P("dp", None),
        P("dp", None),
        P(None, "tensor"),
        P("tensor"),
        P(None, "tensor"),
        P(None, "tensor"),
        P("tensor"),
        P("tensor", None),
        P(),
        P(),
        P(),
        P(None, "tensor"),
        P("tensor"),
        P("tensor", None),
        P(),
        P(),
        P(),
        P("dp", None),
    )
    out_specs = (
        P(("dp", "tensor"), None),
        P(("dp", "tensor"), None),
        P("dp", "tensor"),
        P("tensor"),
        P("dp", "tensor"),
        P("dp", "tensor"),
        P("tensor"),
        P("tensor", "dp"),
        P(("dp", "tensor")),
        P(("dp", "tensor")),
        P(("dp", "tensor")),
        P("dp", "tensor"),
        P("tensor"),
        P("tensor", "dp"),
        P(("dp", "tensor")),
        P(("dp", "tensor")),
        P(("dp", "tensor")),
    )
    return jax.shard_map(
        on_device, mesh=mesh, in_specs=in_specs, out_specs=out_specs, check_vma=False
    )
```

profile of v0, /device:TPU:0, one launch (start us, length us, event | category | flops | bytes accessed | tf_op | source)
XLA Modules:
  0.0 436.8 jit_solution(5846329126646140676)
XLA Ops:
  10.5 52.9 %all-gather.6.cloned.1.call-done = bf16[4,2,192,768]{3,2,1,0:T(8,128)(2,1)} async-done(((bf16[1,2,192,768]{3,2,1,0:T(8,128)(2,1)}), bf16[4,2,192,768]{3,2,1,0:T(8,128)(2,1)}) %all-gather.6.cloned.1.call-update) | async-done | bytes 2359312 | tf_op jit(solution)/shard_map/all_gather | solution.py:193
  63.6 13.1 %all-gather.2 = f32[4,1,1152]{2,1,0:T(1,128)S(1)} all-gather(f32[1,1,1152]{2,1,0:T(1,128)S(1)} %reshape.201), channel_id=2, replica_groups=mesh['dp'=8,'tensor'=4] {'tensor'}, dimensions={0}, use_global_device_ids=true | all-gather | bytes 23040 | tf_op jit(solution)/shard_map/all_gather | solution.py:278
  80.3 2.5 broadcast_select_fusion
  84.4 2.7 convolution_convert_fusion.10.k_ref
  87.1 2.6 add_convert_fusion.1.v_ref
  89.7 2.6 add_convert_fusion.2.q_ref
  92.3 35.2 %shard_map.305 = (bf16[1024,768]{1,0:T(8,128)(2,1)}, f32[1024,128]{1,0:T(8,128)}) custom-call(bf16[1024,768]{1,0:T(8,128)(2,1)} %add_convert_fusion.2.q_ref, bf16[1024,768]{1,0:T(8,128)(2,1)} %convolution_convert_fusion.10.k_ref, bf16[1024,768]{1,0:T(8,128)(2,1)} %add_convert_fusion.1.v_ref, s32[1024,1]{1,0:T(8,128)} %copy.59.segq_ref, ...), custom_call_target="tpu_custom_call" | custom-call | flops 3221225472 | bytes 6291456 | tf_op jit(solution)/shard_map/pallas_call | solution.py:139
  136.5 11.2 %all-gather.8.cloned.1.call-done = bf16[64,96,768]{2,1,0:T(8,128)(2,1)} async-done(((bf16[2,96,768]{2,1,0:T(8,128)(2,1)}), bf16[64,96,768]{2,1,0:T(8,128)(2,1)}) %all-gather.8.cloned.1.call-update) | async-done | bytes 9437200 | tf_op jit(solution)/shard_map/all_gather | solution.py:206
  147.7 4.8 %fusion.59 = (bf16[1,1,8,96,768]{4,3,0,1,2:T(8,128)(2,1)S(1)}, bf16[1,1,8,96,768]{4,3,0,1,2:T(8,128)(2,1)S(1)}, bf16[1,1,8,96,768]{4,3,0,1,2:T(8,128)(2,1)S(1)},...) fusion(bf16[2,4,8,96,768]{4,3,0,1,2:T(8,128)(2,1)} %bitcast.120), kind=kLoop, calls=%fused_computation.160 | loop fusion | bytes 18874368 | tf_op jit(solution)/shard_map/slice | solution.py:316
  152.6 4.0 multiply_convert_fusion.3
  156.5 3.9 multiply_convert_fusion.2
  161.9 3.9 multiply_convert_fusion.1
  167.3 3.9 multiply_convert_fusion
  172.9 2.8 fusion.66
  182.9 8.3 %fusion.8 = bf16[768,3072]{1,0:T(8,128)(2,1)S(1)} fusion(bf16[1024,768]{1,0:T(8,128)(2,1)S(1)} %convert_element_type.157, bf16[1024,768]{0,1:T(8,128)(2,1)} %copy-done.54, bf16[1024,768]{0,1:T(8,128)(2,1)} %copy-done.53, bf16[1024,768]{0,1:T(8,128)(2,1)} %copy-done.52, bf16[1024,768]{0,1:T(8,128)(2,1)S(1)} %copy-done.51), kind=kOutput, calls=%fused_computation.11 | convolution fusion | flops 4859363328 | bytes 12582912 | tf_op jit(solution)/shard_map/dot_general | solution.py:21
  191.2 4.8 %fusion.23 = bf16[1024,768]{0,1:T(8,128)(2,1)S(1)} fusion(f32[1024,768]{0,1:T(8,128)} %get-tuple-element.160, f32[768]{0:T(1024)S(1)} %get-tuple-element.110, bf16[1024,768]{1,0:T(8,128)(2,1)S(1)} %convert_element_type.157, bf16[768,768]{1,0:T(8,128)(2,1)S(1)} %bitcast.147), kind=kOutput, calls=%fused_computation.35 | convolution fusion | flops 1224474624 | bytes 7474176 | tf_op jit(solution)/shard_map/dot_general | solution.py:27
  196.0 3.5 fusion.30
  199.5 3.2 fusion.37
  202.8 3.2 fusion.44
  206.1 3.1 fusion.69
  209.2 3.1 fusion.67
  212.3 3.1 fusion.68
  215.5 15.0 %convolution_convert_fusion = bf16[768,3072]{1,0:T(8,128)(2,1)S(1)} fusion(bf16[1024,768]{1,0:T(8,128)(2,1)} %fusion.46, bf16[1024,768]{0,1:T(8,128)(2,1)S(1)} %fusion.44, bf16[1024,768]{0,1:T(8,128)(2,1)S(1)} %fusion.37, bf16[1024,768]{0,1:T(8,128)(2,1)S(1)} %fusion.30, bf16[1024,768]{0,1:T(8,128)(2,1)S(1)} %fusion.23), kind=kOutput, calls=%fused_computation.10 | convolution fusion | flops 4859363328 | bytes 12582912 | tf_op jit(solution)/shard_map/dot_general | solution.py:21
  239.8 8.7 %add_add_fusion.1 = f32[1024,768]{1,0:T(8,128)} fusion(f32[1024,768]{1,0:T(8,128)} %fusion.69, f32[1024,768]{1,0:T(8,128)} %fusion.68, f32[1024,768]{1,0:T(8,128)} %copy-done.2, f32[1024,768]{1,0:T(8,128)} %fusion.67, bf16[1024,768]{0,1:T(8,128)(2,1)} %copy-done.7, bf16[768,768]{1,0:T(8,128)(2,1)} %bitcast.122), kind=kOutput, calls=%fused_computation.62 | convolution fusion | flops 1211105280 | bytes 18481152 | tf_op jit(solution)/shard_map/dot_general | solution.py:27
  248.7 3.1 multiply_reduce_fusion
  253.4 2.6 convolution_convert_fusion.1.dctx_ref
  258.5 69.0 %shard_map.306 = (bf16[1024,768]{1,0:T(8,128)(2,1)}, bf16[1024,768]{1,0:T(8,128)(2,1)}, bf16[1024,768]{1,0:T(8,128)(2,1)}, bf16[768,3072]{1,0:T(8,128)(2,1)}, f32[8,768]{1,0:T(8,128)}) custom-call(bf16[1024,768]{1,0:T(8,128)(2,1)} %add_convert_fusion.2.q_ref, bf16[1024,768]{1,0:T(8,128)(2,1)} %convolution_convert_fusion.10.k_ref, ...), custom_call_target="tpu_custom_call" | custom-call | flops 11676942336 | bytes 16908288 | tf_op jit(solution)/shard_map/pallas_call | solution.py:163
  328.7 2.9 fusion.70
  335.1 5.8 %convert_reduce_fusion = f32[3072]{0:T(1024)S(1)} fusion(bf16[1024,768]{0,1:T(8,128)(2,1)S(1)} %copy-done.8, bf16[1024,768]{0,1:T(8,128)(2,1)S(1)} %copy-done.23, bf16[1024,768]{0,1:T(8,128)(2,1)S(1)} %copy-done.21, bf16[1024,768]{0,1:T(8,128)(2,1)S(1)} %copy-done.19), kind=kLoop, calls=%fused_computation | loop fusion | flops 28308480 | bytes 6303744 | tf_op jit(solution)/shard_map/reduce_sum | solution.py:337
  340.8 3.1 add_add_fusion
  345.0 39.5 %psum.7 = f32[9216]{0:T(1024)S(1)} all-reduce(f32[9216]{0:T(1024)S(1)} %constant_dynamic-update-slice_fusion.5), channel_id=1, replica_groups=mesh['dp'=8,'tensor'=4] {'dp','tensor'}, use_global_device_ids=true, to_apply=%region_17.18 | all-reduce | flops 9216 | bytes 73728 | tf_op jit(solution)/shard_map/psum | solution.py:358
  389.0 36.8 %reduce-scatter.8.cloned.1.call-done = bf16[96,1,2304]{2,0,1:T(8,128)(2,1)} async-done(((bf16[96,4,2304]{2,0,1:T(8,128)(2,1)}), bf16[96,1,2304]{2,0,1:T(8,128)(2,1)}) %reduce-scatter.8.cloned.1.call-update) | async-done | bytes 442384 | tf_op jit(solution)/shard_map/reduce_scatter | solution.py:235
  (198 shorter events, 56.9 us)
Async XLA Ops:
  7.2 69.7 %copy-start = (s32[4,1024]{1,0:T(4,128)S(1)}, s32[4,1024]{1,0:T(4,128)}, u32[]{:S(2)}) copy-start(s32[4,1024]{1,0:T(4,128)} %param.19) | copy-start | bytes 49156
  7.2 56.2 %copy-start.42 = (f32[768]{0:T(1024)S(1)}, f32[768]{0:T(1024)}, u32[]{:S(2)}) copy-start(f32[768]{0:T(1024)} %param.30) | copy-start | bytes 9220
  7.2 56.2 %copy-start.44 = (f32[192]{0:T(256)S(1)}, f32[192]{0:T(256)}, u32[]{:S(2)}) copy-start(f32[192]{0:T(256)} %param.24) | copy-start | bytes 2308
  7.2 56.2 %copy-start.43 = (f32[192]{0:T(256)S(1)}, f32[192]{0:T(256)}, u32[]{:S(2)}) copy-start(f32[192]{0:T(256)} %param.21) | copy-start | bytes 2308
  7.3 56.2 %all-gather.6.cloned.1.call-start = ((), (), s32[]{:S(2)}) async-start(), calls=%async_computation.3 | async-start | bytes 2949120 | tf_op jit(solution)/shard_map/all_gather | solution.py:193
  9.6 138.1 %all-gather.8.cloned.1.call-start = ((), (), s32[]{:S(2)}) async-start(), calls=%async_computation.7 | async-start | bytes 9732096 | tf_op jit(solution)/shard_map/all_gather | solution.py:206
  10.5 317.0 %reduce-scatter.4.cloned.1.call-start = ((), (), s32[]{:S(2)}) async-start(), calls=%async_computation.4 | async-start | bytes 10616832 | tf_op jit(solution)/shard_map/reduce_scatter | solution.py:217
  63.5 16.8 %collective-permute-start = (bf16[4,2,192,768]{3,2,1,0:T(8,128)(2,1)}, bf16[4,2,192,768]{3,2,1,0:T(8,128)(2,1)}, u32[]{:S(2)}, u32[]{:S(2)}) collective-permute-start(bf16[4,2,192,768]{3,2,1,0:T(8,128)(2,1)} %all-gather.6.cloned.1.call-done), channel_id=1, source_target_pairs={{0,4},{4,0},{8,12},{12,8},{16,20},{20,16},{24,28},{28,24},{1,5},{5... | collective-permute-start | bytes 7077896 | tf_op jit(solution)/shard_map/ppermute | solution.py:196
  80.2 9.5 %copy-start.9 = (bf16[1024,768]{1,0:T(8,128)(2,1)}, bf16[1024,768]{1,0:T(8,128)(2,1)S(1)}, u32[]{:S(2)}) copy-start(bf16[1024,768]{1,0:T(8,128)(2,1)S(1)} %constant_dynamic-slice_fusion.2.x_ref.xall_ref) | copy-start | bytes 4718596
  82.8 48.3 %copy-start.4 = (bf16[4,2,192,768]{3,2,1,0:T(8,128)(2,1)}, bf16[4,2,192,768]{3,2,1,0:T(8,128)(2,1)S(1)}, u32[]{:S(2)}) copy-start(bf16[4,2,192,768]{3,2,1,0:T(8,128)(2,1)S(1)} %get-tuple-element.126) | copy-start | bytes 7077892
  84.4 5.3 %copy-start.27 = (bf16[4,1,192,768]{3,2,1,0:T(8,128)(2,1)}, bf16[4,1,192,768]{3,2,1,0:T(8,128)(2,1)S(1)}, u32[]{:S(2)}) copy-start(bf16[4,1,192,768]{3,2,1,0:T(8,128)(2,1)S(1)} %get-tuple-element.163) | copy-start | bytes 3538948
  127.5 3.6 copy-start.14
  127.6 4.1 copy-start.10
  127.6 4.1 copy-start.40
  147.7 4.8 %copy-start.24 = (bf16[1024,768]{1,0:T(8,128)(2,1)S(1)}, bf16[1024,768]{1,0:T(8,128)(2,1)}, u32[]{:S(2)}) copy-start(bf16[1024,768]{1,0:T(8,128)(2,1)} %fusion.46) | copy-start | bytes 4718596
  152.5 9.3 %copy-start.30 = (bf16[1,1,8,96,768]{4,3,0,1,2:T(8,128)(2,1)}, bf16[1,1,8,96,768]{4,3,0,1,2:T(8,128)(2,1)S(1)}, u32[]{:S(2)}) copy-start(bf16[1,1,8,96,768]{4,3,0,1,2:T(8,128)(2,1)S(1)} %get-tuple-element.122) | copy-start | bytes 3538948
  152.5 14.7 %copy-start.11 = (bf16[1,1,8,96,768]{4,3,0,1,2:T(8,128)(2,1)}, bf16[1,1,8,96,768]{4,3,0,1,2:T(8,128)(2,1)S(1)}, u32[]{:S(2)}) copy-start(bf16[1,1,8,96,768]{4,3,0,1,2:T(8,128)(2,1)S(1)} %get-tuple-element.120) | copy-start | bytes 3538948
  152.5 18.6 %copy-start.32 = (bf16[1,1,8,96,768]{4,3,0,1,2:T(8,128)(2,1)}, bf16[1,1,8,96,768]{4,3,0,1,2:T(8,128)(2,1)S(1)}, u32[]{:S(2)}) copy-start(bf16[1,1,8,96,768]{4,3,0,1,2:T(8,128)(2,1)S(1)} %get-tuple-element.119) | copy-start | bytes 3538948
  156.5 16.3 %copy-start.50 = (bf16[1024,768]{0,1:T(8,128)(2,1)}, bf16[1024,768]{0,1:T(8,128)(2,1)S(1)}, u32[]{:S(2)}) copy-start(bf16[1024,768]{0,1:T(8,128)(2,1)S(1)} %get-tuple-element.159) | copy-start | bytes 4718596
  172.8 3.3 slice-start
  191.2 4.8 %copy-start.49 = (f32[1024,768]{0,1:T(8,128)S(1)}, f32[1024,768]{0,1:T(8,128)}, u32[]{:S(2)}) copy-start(f32[1024,768]{0,1:T(8,128)} %get-tuple-element.158) | copy-start | bytes 9437188
  196.0 19.5 %copy-start.18 = (bf16[1024,768]{0,1:T(8,128)(2,1)}, bf16[1024,768]{0,1:T(8,128)(2,1)S(1)}, u32[]{:S(2)}) copy-start(bf16[1024,768]{0,1:T(8,128)(2,1)S(1)} %fusion.23) | copy-start | bytes 4718596
  196.0 3.5 copy-start.47
  199.5 16.0 %copy-start.20 = (bf16[1024,768]{0,1:T(8,128)(2,1)}, bf16[1024,768]{0,1:T(8,128)(2,1)S(1)}, u32[]{:S(2)}) copy-start(bf16[1024,768]{0,1:T(8,128)(2,1)S(1)} %fusion.30) | copy-start | bytes 4718596
  202.8 12.7 %copy-start.22 = (bf16[1024,768]{0,1:T(8,128)(2,1)}, bf16[1024,768]{0,1:T(8,128)(2,1)S(1)}, u32[]{:S(2)}) copy-start(bf16[1024,768]{0,1:T(8,128)(2,1)S(1)} %fusion.37) | copy-start | bytes 4718596
  206.1 9.4 %copy-start.7 = (bf16[1024,768]{0,1:T(8,128)(2,1)}, bf16[1024,768]{0,1:T(8,128)(2,1)S(1)}, u32[]{:S(2)}) copy-start(bf16[1024,768]{0,1:T(8,128)(2,1)S(1)} %fusion.44) | copy-start | bytes 4718596
  248.6 135.9 %reduce-scatter.6.cloned.1.call-start = ((), (), s32[]{:S(2)}) async-start(), calls=%async_computation.5 | async-start | bytes 5308416 | tf_op jit(solution)/shard_map/reduce_scatter | solution.py:217
  327.5 98.3 %reduce-scatter.8.cloned.1.call-start = ((), (), s32[]{:S(2)}) async-start(), calls=%async_computation.6 | async-start | bytes 2211840 | tf_op jit(solution)/shard_map/reduce_scatter | solution.py:235
  335.0 5.8 %copy-start.6 = (f32[1024,768]{1,0:T(8,128)S(1)}, f32[1024,768]{1,0:T(8,128)}, u32[]{:S(2)}) copy-start(f32[1024,768]{1,0:T(8,128)} %copy-done.5) | copy-start | bytes 9437188
  335.0 5.8 %copy-start.13 = (bf16[4,1,192,768]{3,2,1,0:T(8,128)(2,1)S(1)}, bf16[4,1,192,768]{3,2,1,0:T(8,128)(2,1)}, u32[]{:S(2)}) copy-start(bf16[4,1,192,768]{3,2,1,0:T(8,128)(2,1)} %copy-done.12) | copy-start | bytes 3538948
  335.1 5.8 %copy-start.17 = (bf16[1024,768]{1,0:T(8,128)(2,1)S(1)}, bf16[1024,768]{1,0:T(8,128)(2,1)}, u32[]{:S(2)}) copy-start(bf16[1024,768]{1,0:T(8,128)(2,1)} %get-tuple-element.44) | copy-start | bytes 4718596
  385.6 44.5 %copy-start.1 = (s32[4,1024]{1,0:T(4,128)S(1)}, s32[4,1024]{1,0:T(4,128)}, u32[]{:S(2)}) copy-start(s32[4,1024]{1,0:T(4,128)} %param.19) | copy-start | bytes 49156
  (31 other events, 70.7 us)
Sparse Core Ops, SparseCore 0:
  10.2 53.1 all-gather.5
  66.8 80.8 all-gather.7
  248.7 75.0 reduce-scatter.3
  327.6 53.8 reduce-scatter.5
  387.1 38.5 reduce-scatter.7
where the time goes:
time: 441 us; the launch traced here: 437 us
  matrix products  106 us (24%)
  Pallas kernels  104 us (24%)
  waiting for transfers between devices  101 us (23%)
  blocking collectives  52.6 us (12%)
  local copies, waits for them, and re-layouts  30.6 us (7%)
  other arithmetic  27.3 us (6%)
  between operations  15 us (3%)
    pallas_call x1, Pallas kernels, attention_backward(): pl.pallas_call(functools.partial(attn_bwd_kernel, parts), out_shape=tuple...  69 us
    all_gather x1, waiting for transfers between devices, gather_shards(): gathered = lax.all_gather(mine, 'tensor', axis=0, tiled=False)  52.9 us
    dot_general x12, matrix products, contract_last(): lax.dot_general(left_side, right_side, (((1,), (1,)), ((), ())), preferre...  43.3 us
    psum x1, blocking collectives, on_device(): lax.psum(jnp.concatenate([grad_query_bias, grad_value_bias, grad_up_bias,...  39.5 us
    reduce_scatter x1, waiting for transfers between devices, scatter_parts(): lax.psum_scatter(joined, 'tensor', scatter_dimension=1, tiled=True)[:, 0]  36.8 us
    dot_general x15, matrix products, product(): return jnp.dot(left_side, right_side, preferred_element_type=jnp.float32)  36.8 us
    pallas_call x1, Pallas kernels, attention_forward(): pl.pallas_call(attn_fwd_kernel, out_shape=(jax.ShapeDtypeStruct((length,...  35.2 us
    dot_general x3, matrix products, contract_rows(): lax.dot_general(left_side, right_side, (((0,), (0,)), ((), ())), preferre...  25.7 us
  transfers between devices with their start and end apart: 6, of which 3 were waited for; matrix products, arithmetic and copies ran while one was open for 12% of the time, Pallas kernels for 24%

commit v1 on v0

--- a/solution.py
+++ b/solution.py
@@ -185,17 +185,27 @@
     )(queries, key_side, value_proj, grad_context, segq, segk, stats, inputs, inputs, out_t)
 
 
-def gather_shards(first_pieces, second_pieces, after=None):
+def gather_shards(first_pieces, second_pieces, extra):
     dp_count = lax.axis_size("dp")
+    part_count = lax.axis_size("tensor")
+    part_id = lax.axis_index("tensor")
     core = lax.rem(lax.axis_index("dp"), 2)
     first, second = jnp.stack(first_pieces), jnp.stack(second_pieces)
     mine = jnp.where(core == 0, first, second)
-    gathered = lax.all_gather(mine, "tensor", axis=0, tiled=False)
-    if after is not None:
-        gathered, after = lax.optimization_barrier((gathered, after))
+
+    def around(value):
+        received = [value]
+        for shift in range(1, part_count):
+            perm = [(i, (i + shift) % part_count) for i in range(part_count)]
+            received.append(lax.ppermute(value, "tensor", perm=perm))
+        order = lax.rem(part_id - jnp.arange(part_count) + part_count, part_count)
+        return jnp.take(jnp.stack(received), order, axis=0)
+
+    gathered = around(mine)
+    extras = around(extra)
     other = lax.ppermute(gathered, "dp", perm=[(i, i ^ 1) for i in range(dp_count)])
     halves = (jnp.where(core == 0, gathered, other), jnp.where(core == 0, other, gathered))
-    return [half[:, index] for half in halves for index in range(half.shape[1])]
+    return [half[:, index] for half in halves for index in range(half.shape[1])], extras
 
 
 def gather_pieces(pieces, after):
@@ -272,11 +282,10 @@
         jnp.float32
     )
 
-    qt_sh, kt_sh, vt_sh, o_sh = gather_shards(
-        [query_weight.T, key_weight.T], [value_weight.T, output_weight]
-    )
-    bias_sh = lax.all_gather(
-        jnp.concatenate([query_bias, value_bias, up_bias]), "tensor", axis=0, tiled=False
+    (qt_sh, kt_sh, vt_sh, o_sh), bias_sh = gather_shards(
+        [query_weight.T, key_weight.T],
+        [value_weight.T, output_weight],
+        jnp.concatenate([query_bias, value_bias, up_bias]),
     )
     head_width = query_bias.shape[0]
     qb = bias_sh[:, :head_width].reshape(-1)

time: 441 us -> 452 us (1.025)
  starting transfers between devices: 0.2 us -> 15.4 us
  blocking collectives: 52.6 us -> 39.4 us
    ppermute x0 -> x6, waiting for transfers between devices: none -> 64.2 us  [around(): received.append(lax.ppermute(value, 'tensor', perm=perm))]
    all_gather x1 -> x0, waiting for transfers between devices: 52.9 us -> none  [gather_shards(): gathered = lax.all_gather(mine, 'tensor', axis=0, tiled=False)]
    ppermute x0 -> x6, starting transfers between devices: none -> 15.2 us  [around(): received.append(lax.ppermute(value, 'tensor', perm=perm))]
    all_gather x1 -> x0, blocking collectives: 13.1 us -> none  [on_device(): lax.all_gather(jnp.concatenate([query_bias, value_bias, up_bias]), 'tenso...]
    all_gather x1, waiting for transfers between devices: 11.2 us -> 0.01 us  [gather_pieces(): gathered = lax.all_gather(own, ('dp', 'tensor'), axis=0, tiled=False)]
    unnamed x132 -> x130, local copies, waits for them, and re-layouts: 15.5 us -> 16 us
  transfers between devices with their start and end apart: 6 -> 11, of which waited for: 3 -> 3; matrix products, arithmetic and copies ran while one was open for 12% -> 13% of each run, Pallas kernels for 24% -> 23%
where the time goes in v1:
time: 452 us; the launch traced here: 446 us
  matrix products  105 us (23%)
  Pallas kernels  104 us (23%)
  waiting for transfers between devices  101 us (22%)
  blocking collectives  39.4 us (9%)
  local copies, waits for them, and re-layouts  34.6 us (8%)
  other arithmetic  31.2 us (7%)
  starting transfers between devices  15.4 us (3%)
  between operations  15.3 us (3%)
    pallas_call x1, Pallas kernels, attention_backward(): pl.pallas_call(functools.partial(attn_bwd_kernel, parts), out_shape=tuple...  69 us
    ppermute x6, waiting for transfers between devices, around(): received.append(lax.ppermute(value, 'tensor', perm=perm))  64.2 us
    dot_general x12, matrix products, contract_last(): lax.dot_general(left_side, right_side, (((1,), (1,)), ((), ())), preferre...  43.5 us
    psum x1, blocking collectives, on_device(): lax.psum(jnp.concatenate([grad_query_bias, grad_value_bias, grad_up_bias,...  39.4 us
    reduce_scatter x1, waiting for transfers between devices, scatter_parts(): lax.psum_scatter(joined, 'tensor', scatter_dimension=1, tiled=True)[:, 0]  36.6 us
    dot_general x15, matrix products, product(): return jnp.dot(left_side, right_side, preferred_element_type=jnp.float32)  36.4 us
    pallas_call x1, Pallas kernels, attention_forward(): pl.pallas_call(attn_fwd_kernel, out_shape=(jax.ShapeDtypeStruct((length,...  35.4 us
    dot_general x3, matrix products, contract_rows(): lax.dot_general(left_side, right_side, (((0,), (0,)), ((), ())), preferre...  25.6 us
  transfers between devices with their start and end apart: 11, of which 3 were waited for; matrix products, arithmetic and copies ran while one was open for 13% of the time, Pallas kernels for 23%

profile of v1, /device:TPU:0, one launch (start us, length us, event | category | flops | bytes accessed | tf_op | source)
XLA Modules:
  0.0 446.4 jit_solution(13376194070233033363)
XLA Ops:
  10.1 5.0 %collective-permute-start.2 = (bf16[2,192,768]{2,1,0:T(8,128)(2,1)}, bf16[2,192,768]{2,1,0:T(8,128)(2,1)S(1)}, u32[]{:S(2)}, u32[]{:S(2)}) collective-permute-start(bf16[2,192,768]{2,1,0:T(8,128)(2,1)} %maximum_select_fusion.1), channel_id=1, source_target_pairs={{0,3},{1,0},{2,1},{3,2},{4,7},{5,4},{6,5},{7,6},{8,11},{9,8},{10,9... | collective-permute-start | bytes 1769480 | tf_op jit(solution)/shard_map/ppermute | solution.py:200
  16.4 17.9 %collective-permute-done.2 = bf16[2,192,768]{2,1,0:T(8,128)(2,1)S(1)} collective-permute-done((bf16[2,192,768]{2,1,0:T(8,128)(2,1)}, bf16[2,192,768]{2,1,0:T(8,128)(2,1)S(1)}, u32[]{:S(2)}, u32[]{:S(2)}) %collective-permute-start.2) | collective-permute-done | bytes 589856 | tf_op jit(solution)/shard_map/ppermute | solution.py:200
  34.3 46.2 %collective-permute-done.1 = bf16[2,192,768]{2,1,0:T(8,128)(2,1)S(1)} collective-permute-done((bf16[2,192,768]{2,1,0:T(8,128)(2,1)}, bf16[2,192,768]{2,1,0:T(8,128)(2,1)S(1)}, u32[]{:S(2)}, u32[]{:S(2)}) %collective-permute-start.1) | collective-permute-done | bytes 589856 | tf_op jit(solution)/shard_map/ppermute | solution.py:200
  80.5 2.8 pad_maximum_fusion.1
  87.5 7.2 %collective-permute-start.5 = (f32[1152]{0:T(1024)S(1)}, f32[1152]{0:T(1024)S(1)}, u32[]{:S(2)}, u32[]{:S(2)}) collective-permute-start(f32[1152]{0:T(1024)S(1)} %concatenate.32), channel_id=1, source_target_pairs={{0,2},{1,3},{2,0},{3,1},{4,6},{5,7},{6,4},{7,5},{8,10},{9,11},{10,... | collective-permute-start | bytes 13832 | tf_op jit(solution)/shard_map/ppermute | solution.py:200
  97.2 2.7 constant_dynamic-slice_fusion.2.x_ref.xall_ref
  106.6 2.7 convolution_convert_fusion.10.k_ref
  111.9 2.6 add_convert_fusion.2.q_ref
  114.5 35.4 %shard_map.305 = (bf16[1024,768]{1,0:T(8,128)(2,1)}, f32[1024,128]{1,0:T(8,128)}) custom-call(bf16[1024,768]{1,0:T(8,128)(2,1)} %add_convert_fusion.2.q_ref, bf16[1024,768]{1,0:T(8,128)(2,1)} %convolution_convert_fusion.10.k_ref, bf16[1024,768]{1,0:T(8,128)(2,1)} %add_convert_fusion.1.v_ref, s32[1024,1]{1,0:T(8,128)} %copy.59.segq_ref, ...), custom_call_target="tpu_custom_call" | custom-call | flops 3221225472 | bytes 6291456 | tf_op jit(solution)/shard_map/pallas_call | solution.py:139
  159.9 4.4 fusion.62
  164.4 4.0 multiply_convert_fusion.3
  168.4 3.8 multiply_convert_fusion.2
  173.7 3.9 multiply_convert_fusion.1
  179.1 3.9 multiply_convert_fusion
  184.7 2.8 fusion.69
  194.0 8.4 %fusion.8 = bf16[768,3072]{1,0:T(8,128)(2,1)S(1)} fusion(bf16[1024,768]{1,0:T(8,128)(2,1)S(1)} %convert_element_type.157, bf16[1024,768]{0,1:T(8,128)(2,1)} %copy-done.54, bf16[1024,768]{0,1:T(8,128)(2,1)} %copy-done.53, bf16[1024,768]{0,1:T(8,128)(2,1)} %copy-done.52, bf16[1024,768]{0,1:T(8,128)(2,1)S(1)} %get-tuple-element.159), kind=kOutput, calls=%fused_computation.13 | convolution fusion | flops 4859363328 | bytes 12582912 | tf_op jit(solution)/shard_map/dot_general | solution.py:21
  202.4 4.8 %fusion.23 = bf16[1024,768]{0,1:T(8,128)(2,1)S(1)} fusion(f32[1024,768]{0,1:T(8,128)} %get-tuple-element.160, f32[768]{0:T(1024)S(1)} %get-tuple-element.110, bf16[1024,768]{1,0:T(8,128)(2,1)S(1)} %convert_element_type.157, bf16[768,768]{1,0:T(8,128)(2,1)S(1)} %bitcast.156), kind=kOutput, calls=%fused_computation.37 | convolution fusion | flops 1224474624 | bytes 7474176 | tf_op jit(solution)/shard_map/dot_general | solution.py:27
  207.2 3.6 fusion.30
  210.9 3.2 fusion.37
  214.2 3.2 fusion.44
  217.4 3.1 fusion.72
  220.6 3.1 fusion.70
  223.7 3.1 fusion.71
  226.8 14.7 %convolution_convert_fusion = bf16[768,3072]{1,0:T(8,128)(2,1)S(1)} fusion(bf16[1024,768]{1,0:T(8,128)(2,1)} %fusion.46, bf16[1024,768]{0,1:T(8,128)(2,1)S(1)} %fusion.44, bf16[1024,768]{0,1:T(8,128)(2,1)S(1)} %fusion.37, bf16[1024,768]{0,1:T(8,128)(2,1)S(1)} %fusion.30, bf16[1024,768]{0,1:T(8,128)(2,1)S(1)} %fusion.23), kind=kOutput, calls=%fused_computation.12 | convolution fusion | flops 4859363328 | bytes 12582912 | tf_op jit(solution)/shard_map/dot_general | solution.py:21
  251.0 8.7 %add_add_fusion.1 = f32[1024,768]{1,0:T(8,128)} fusion(f32[1024,768]{1,0:T(8,128)} %fusion.72, f32[1024,768]{1,0:T(8,128)} %fusion.71, f32[1024,768]{1,0:T(8,128)} %copy-done.2, f32[1024,768]{1,0:T(8,128)} %fusion.70, bf16[1024,768]{0,1:T(8,128)(2,1)} %copy-done.7, bf16[768,768]{1,0:T(8,128)(2,1)} %bitcast.131), kind=kOutput, calls=%fused_computation.64 | convolution fusion | flops 1211105280 | bytes 18481152 | tf_op jit(solution)/shard_map/dot_general | solution.py:27
  259.8 3.1 multiply_reduce_fusion
  264.2 2.6 convolution_convert_fusion.1.dctx_ref
  269.4 69.0 %shard_map.306 = (bf16[1024,768]{1,0:T(8,128)(2,1)}, bf16[1024,768]{1,0:T(8,128)(2,1)}, bf16[1024,768]{1,0:T(8,128)(2,1)}, bf16[768,3072]{1,0:T(8,128)(2,1)}, f32[8,768]{1,0:T(8,128)}) custom-call(bf16[1024,768]{1,0:T(8,128)(2,1)} %add_convert_fusion.2.q_ref, bf16[1024,768]{1,0:T(8,128)(2,1)} %convolution_convert_fusion.10.k_ref, ...), custom_call_target="tpu_custom_call" | custom-call | flops 11676942336 | bytes 16908288 | tf_op jit(solution)/shard_map/pallas_call | solution.py:163
  344.8 5.8 %convert_reduce_fusion = f32[3072]{0:T(1024)S(1)} fusion(bf16[1024,768]{0,1:T(8,128)(2,1)S(1)} %copy-done.8, bf16[1024,768]{0,1:T(8,128)(2,1)S(1)} %copy-done.22, bf16[1024,768]{0,1:T(8,128)(2,1)S(1)} %copy-done.20, bf16[1024,768]{0,1:T(8,128)(2,1)S(1)} %copy-done.18), kind=kLoop, calls=%fused_computation.2 | loop fusion | flops 28308480 | bytes 6303744 | tf_op jit(solution)/shard_map/reduce_sum | solution.py:346
  350.6 3.1 add_add_fusion
  354.7 39.4 %psum.7 = f32[9216]{0:T(1024)S(1)} all-reduce(f32[9216]{0:T(1024)S(1)} %constant_dynamic-update-slice_fusion.5), channel_id=1, replica_groups=mesh['dp'=8,'tensor'=4] {'dp','tensor'}, use_global_device_ids=true, to_apply=%region_17.18 | all-reduce | flops 9216 | bytes 73728 | tf_op jit(solution)/shard_map/psum | solution.py:367
  398.6 36.6 %reduce-scatter.8.cloned.1.call-done = bf16[96,1,2304]{2,0,1:T(8,128)(2,1)} async-done(((bf16[96,4,2304]{2,0,1:T(8,128)(2,1)}), bf16[96,1,2304]{2,0,1:T(8,128)(2,1)}) %reduce-scatter.8.cloned.1.call-update) | async-done | bytes 442384 | tf_op jit(solution)/shard_map/reduce_scatter | solution.py:245
  (218 shorter events, 70.3 us)
Async XLA Ops:
  7.2 89.5 %copy-start = (s32[4,1024]{1,0:T(4,128)S(1)}, s32[4,1024]{1,0:T(4,128)}, u32[]{:S(2)}) copy-start(s32[4,1024]{1,0:T(4,128)} %param.19) | copy-start | bytes 49156
  7.2 152.7 %all-gather.3.cloned.1.call-start = ((), (), s32[]{:S(2)}) async-start(), calls=%async_computation.6 | async-start | bytes 9732096 | tf_op jit(solution)/shard_map/all_gather | solution.py:216
  9.1 329.3 %reduce-scatter.4.cloned.1.call-start = ((), (), s32[]{:S(2)}) async-start(), calls=%async_computation.3 | async-start | bytes 10616832 | tf_op jit(solution)/shard_map/reduce_scatter | solution.py:227
  10.1 24.1 %collective-permute-start.2 = (bf16[2,192,768]{2,1,0:T(8,128)(2,1)}, bf16[2,192,768]{2,1,0:T(8,128)(2,1)S(1)}, u32[]{:S(2)}, u32[]{:S(2)}) collective-permute-start(bf16[2,192,768]{2,1,0:T(8,128)(2,1)} %maximum_select_fusion.1), channel_id=1, source_target_pairs={{0,3},{1,0},{2,1},{3,2},{4,7},{5,4},{6,5},{7,6},{8,11},{9,8},{10,9... | collective-permute-start | bytes 1769480 | tf_op jit(solution)/shard_map/ppermute | solution.py:200
  15.2 65.3 %collective-permute-start.1 = (bf16[2,192,768]{2,1,0:T(8,128)(2,1)}, bf16[2,192,768]{2,1,0:T(8,128)(2,1)S(1)}, u32[]{:S(2)}, u32[]{:S(2)}) collective-permute-start(bf16[2,192,768]{2,1,0:T(8,128)(2,1)} %maximum_select_fusion.1), channel_id=1, source_target_pairs={{0,2},{1,3},{2,0},{3,1},{4,6},{5,7},{6,4},{7,5},{8,10},{9,11},{10,... | collective-permute-start | bytes 1769480 | tf_op jit(solution)/shard_map/ppermute | solution.py:200
  15.2 65.3 %collective-permute-start = (bf16[2,192,768]{2,1,0:T(8,128)(2,1)}, bf16[2,192,768]{2,1,0:T(8,128)(2,1)}, u32[]{:S(2)}, u32[]{:S(2)}) collective-permute-start(bf16[2,192,768]{2,1,0:T(8,128)(2,1)} %maximum_select_fusion.1), channel_id=1, source_target_pairs={{0,1},{1,2},{2,3},{3,0},{4,5},{5,6},{6,7},{7,4},{8,9},{9,10},{10,1... | collective-permute-start | bytes 1769480 | tf_op jit(solution)/shard_map/ppermute | solution.py:200
  87.4 14.6 %collective-permute-start.3 = (bf16[4,2,192,768]{3,2,1,0:T(8,128)(2,1)}, bf16[4,2,192,768]{3,2,1,0:T(8,128)(2,1)}, u32[]{:S(2)}, u32[]{:S(2)}) collective-permute-start(bf16[4,2,192,768]{3,2,1,0:T(8,128)(2,1)} %broadcast_select_fusion), channel_id=1, source_target_pairs={{0,4},{4,0},{8,12},{12,8},{16,20},{20,16},{24,28},{28,24},{1,5},{5... | collective-permute-start | bytes 7077896 | tf_op jit(solution)/shard_map/ppermute | solution.py:206
  87.5 13.5 %collective-permute-start.6 = (f32[1152]{0:T(1024)S(1)}, f32[1152]{0:T(1024)S(1)}, u32[]{:S(2)}, u32[]{:S(2)}) collective-permute-start(f32[1152]{0:T(1024)S(1)} %concatenate.32), channel_id=1, source_target_pairs={{0,3},{1,0},{2,1},{3,2},{4,7},{5,4},{6,5},{7,6},{8,11},{9,8},{10,9... | collective-permute-start | bytes 13832 | tf_op jit(solution)/shard_map/ppermute | solution.py:200
  87.5 13.5 %collective-permute-start.5 = (f32[1152]{0:T(1024)S(1)}, f32[1152]{0:T(1024)S(1)}, u32[]{:S(2)}, u32[]{:S(2)}) collective-permute-start(f32[1152]{0:T(1024)S(1)} %concatenate.32), channel_id=1, source_target_pairs={{0,2},{1,3},{2,0},{3,1},{4,6},{5,7},{6,4},{7,5},{8,10},{9,11},{10,... | collective-permute-start | bytes 13832 | tf_op jit(solution)/shard_map/ppermute | solution.py:200
  94.7 6.3 %collective-permute-start.4 = (f32[1152]{0:T(1024)S(1)}, f32[1152]{0:T(1024)S(1)}, u32[]{:S(2)}, u32[]{:S(2)}) collective-permute-start(f32[1152]{0:T(1024)S(1)} %concatenate.32), channel_id=1, source_target_pairs={{0,1},{1,2},{2,3},{3,0},{4,5},{5,6},{6,7},{7,4},{8,9},{9,10},{10,1... | collective-permute-start | bytes 13832 | tf_op jit(solution)/shard_map/ppermute | solution.py:200
  105.9 3.4 copy-start.24
  105.9 3.4 copy-start.12
  105.9 6.0 %copy-start.26 = (bf16[4,1,192,768]{3,2,1,0:T(8,128)(2,1)}, bf16[4,1,192,768]{3,2,1,0:T(8,128)(2,1)S(1)}, u32[]{:S(2)}) copy-start(bf16[4,1,192,768]{3,2,1,0:T(8,128)(2,1)S(1)} %get-tuple-element.163) | copy-start | bytes 3538948
  149.9 3.7 copy-start.14
  149.9 5.2 %copy-start.10 = (bf16[1024,768]{1,0:T(8,128)(2,1)S(1)}, bf16[1024,768]{1,0:T(8,128)(2,1)}, u32[]{:S(2)}) copy-start(bf16[1024,768]{1,0:T(8,128)(2,1)} %constant_dynamic-slice_fusion.2.x_ref.xall_ref) | copy-start | bytes 4718596
  149.9 5.2 %copy-start.41 = (f32[768]{0:T(1024)S(1)}, f32[768]{0:T(1024)}, u32[]{:S(2)}) copy-start(f32[768]{0:T(1024)} %param.26) | copy-start | bytes 9220
  159.9 4.5 copy-start.23
  164.3 9.3 %copy-start.29 = (bf16[1,1,8,96,768]{4,3,0,1,2:T(8,128)(2,1)}, bf16[1,1,8,96,768]{4,3,0,1,2:T(8,128)(2,1)S(1)}, u32[]{:S(2)}) copy-start(bf16[1,1,8,96,768]{4,3,0,1,2:T(8,128)(2,1)S(1)} %get-tuple-element.122) | copy-start | bytes 3538948
  164.4 14.7 %copy-start.11 = (bf16[1,1,8,96,768]{4,3,0,1,2:T(8,128)(2,1)}, bf16[1,1,8,96,768]{4,3,0,1,2:T(8,128)(2,1)S(1)}, u32[]{:S(2)}) copy-start(bf16[1,1,8,96,768]{4,3,0,1,2:T(8,128)(2,1)S(1)} %get-tuple-element.120) | copy-start | bytes 3538948
  164.4 18.6 %copy-start.31 = (bf16[1,1,8,96,768]{4,3,0,1,2:T(8,128)(2,1)}, bf16[1,1,8,96,768]{4,3,0,1,2:T(8,128)(2,1)S(1)}, u32[]{:S(2)}) copy-start(bf16[1,1,8,96,768]{4,3,0,1,2:T(8,128)(2,1)S(1)} %get-tuple-element.119) | copy-start | bytes 3538948
  202.3 4.8 %copy-start.51 = (f32[1024,768]{0,1:T(8,128)S(1)}, f32[1024,768]{0,1:T(8,128)}, u32[]{:S(2)}) copy-start(f32[1024,768]{0,1:T(8,128)} %get-tuple-element.158) | copy-start | bytes 9437188
  207.1 19.7 %copy-start.17 = (bf16[1024,768]{0,1:T(8,128)(2,1)}, bf16[1024,768]{0,1:T(8,128)(2,1)S(1)}, u32[]{:S(2)}) copy-start(bf16[1024,768]{0,1:T(8,128)(2,1)S(1)} %fusion.23) | copy-start | bytes 4718596
  207.2 3.7 copy-start.49
  210.8 16.0 %copy-start.19 = (bf16[1024,768]{0,1:T(8,128)(2,1)}, bf16[1024,768]{0,1:T(8,128)(2,1)S(1)}, u32[]{:S(2)}) copy-start(bf16[1024,768]{0,1:T(8,128)(2,1)S(1)} %fusion.30) | copy-start | bytes 4718596
  214.1 12.7 %copy-start.21 = (bf16[1024,768]{0,1:T(8,128)(2,1)}, bf16[1024,768]{0,1:T(8,128)(2,1)S(1)}, u32[]{:S(2)}) copy-start(bf16[1024,768]{0,1:T(8,128)(2,1)S(1)} %fusion.37) | copy-start | bytes 4718596
  217.4 9.4 %copy-start.7 = (bf16[1024,768]{0,1:T(8,128)(2,1)}, bf16[1024,768]{0,1:T(8,128)(2,1)S(1)}, u32[]{:S(2)}) copy-start(bf16[1024,768]{0,1:T(8,128)(2,1)S(1)} %fusion.44) | copy-start | bytes 4718596
  259.7 134.3 %reduce-scatter.6.cloned.1.call-start = ((), (), s32[]{:S(2)}) async-start(), calls=%async_computation.4 | async-start | bytes 5308416 | tf_op jit(solution)/shard_map/reduce_scatter | solution.py:227
  338.4 96.7 %reduce-scatter.8.cloned.1.call-start = ((), (), s32[]{:S(2)}) async-start(), calls=%async_computation.5 | async-start | bytes 2211840 | tf_op jit(solution)/shard_map/reduce_scatter | solution.py:245
  344.7 5.8 %copy-start.6 = (f32[1024,768]{1,0:T(8,128)S(1)}, f32[1024,768]{1,0:T(8,128)}, u32[]{:S(2)}) copy-start(f32[1024,768]{1,0:T(8,128)} %copy-done.5) | copy-start | bytes 9437188
  344.7 5.8 %copy-start.13 = (bf16[4,1,192,768]{3,2,1,0:T(8,128)(2,1)S(1)}, bf16[4,1,192,768]{3,2,1,0:T(8,128)(2,1)}, u32[]{:S(2)}) copy-start(bf16[4,1,192,768]{3,2,1,0:T(8,128)(2,1)} %copy-done.12) | copy-start | bytes 3538948
  344.8 5.8 %copy-start.16 = (bf16[1024,768]{1,0:T(8,128)(2,1)S(1)}, bf16[1024,768]{1,0:T(8,128)(2,1)}, u32[]{:S(2)}) copy-start(bf16[1024,768]{1,0:T(8,128)(2,1)} %get-tuple-element.44) | copy-start | bytes 4718596
  395.2 44.3 %copy-start.1 = (s32[4,1024]{1,0:T(4,128)S(1)}, s32[4,1024]{1,0:T(4,128)}, u32[]{:S(2)}) copy-start(s32[4,1024]{1,0:T(4,128)} %param.19) | copy-start | bytes 49156
  (36 other events, 73.5 us)
Sparse Core Ops, SparseCore 0:
  11.5 113.2 all-gather.2
  259.8 76.0 reduce-scatter.3
  339.4 54.5 reduce-scatter.5
  396.7 38.4 reduce-scatter.7

commit v2 on v0

--- a/solution.py
+++ b/solution.py
@@ -371,6 +371,9 @@
         ),
         ("dp", "tensor"),
     )
+    small, query_low, key_low, value_low = lax.optimization_barrier(
+        (small, query_low, key_low, value_low)
+    )
     input_grad = (
         attn_grad
         + product(query_low, qt_full)

time: 441 us -> 441 us (level)
    unnamed x132 -> x124, local copies, waits for them, and re-layouts: 15.5 us -> 15.5 us
  transfers between devices with their start and end apart: 6 -> 6, of which waited for: 3 -> 3; matrix products, arithmetic and copies ran while one was open for 12% -> 11% of each run, Pallas kernels for 24% -> 24%
where the time goes in v2:
time: 441 us; the launch traced here: 436 us
  matrix products  106 us (24%)
  Pallas kernels  104 us (24%)
  waiting for transfers between devices  101 us (23%)
  blocking collectives  52.3 us (12%)
  local copies, waits for them, and re-layouts  31.8 us (7%)
  other arithmetic  25.5 us (6%)
  between operations  15 us (3%)
    pallas_call x1, Pallas kernels, attention_backward(): pl.pallas_call(functools.partial(attn_bwd_kernel, parts), out_shape=tuple...  69 us
    all_gather x1, waiting for transfers between devices, gather_shards(): gathered = lax.all_gather(mine, 'tensor', axis=0, tiled=False)  52.9 us
    dot_general x12, matrix products, contract_last(): lax.dot_general(left_side, right_side, (((1,), (1,)), ((), ())), preferre...  43.3 us
    psum x1, blocking collectives, on_device(): lax.psum(jnp.concatenate([grad_query_bias, grad_value_bias, grad_up_bias,...  39.2 us
    dot_general x15, matrix products, product(): return jnp.dot(left_side, right_side, preferred_element_type=jnp.float32)  37.1 us
    reduce_scatter x1, waiting for transfers between devices, scatter_parts(): lax.psum_scatter(joined, 'tensor', scatter_dimension=1, tiled=True)[:, 0]  36.8 us
    pallas_call x1, Pallas kernels, attention_forward(): pl.pallas_call(attn_fwd_kernel, out_shape=(jax.ShapeDtypeStruct((length,...  35.2 us
    dot_general x3, matrix products, contract_rows(): lax.dot_general(left_side, right_side, (((0,), (0,)), ((), ())), preferre...  25.8 us
  transfers between devices with their start and end apart: 6, of which 3 were waited for; matrix products, arithmetic and copies ran while one was open for 11% of the time, Pallas kernels for 24%

profile of v2, /device:TPU:0, one launch (start us, length us, event | category | flops | bytes accessed | tf_op | source)
XLA Modules:
  0.0 436.4 jit_solution(9719989019261793898)
XLA Ops:
  10.5 52.9 %all-gather.6.cloned.1.call-done = bf16[4,2,192,768]{3,2,1,0:T(8,128)(2,1)} async-done(((bf16[1,2,192,768]{3,2,1,0:T(8,128)(2,1)}), bf16[4,2,192,768]{3,2,1,0:T(8,128)(2,1)}) %all-gather.6.cloned.1.call-update) | async-done | bytes 2359312 | tf_op jit(solution)/shard_map/all_gather | solution.py:193
  63.6 13.1 %all-gather.2 = f32[4,1,1152]{2,1,0:T(1,128)S(1)} all-gather(f32[1,1,1152]{2,1,0:T(1,128)S(1)} %reshape.201), channel_id=2, replica_groups=mesh['dp'=8,'tensor'=4] {'tensor'}, dimensions={0}, use_global_device_ids=true | all-gather | bytes 23040 | tf_op jit(solution)/shard_map/all_gather | solution.py:278
  84.4 2.7 convolution_convert_fusion.10.k_ref
  87.1 2.6 add_convert_fusion.1.v_ref
  89.7 2.6 add_convert_fusion.2.q_ref
  92.3 35.2 %shard_map.305 = (bf16[1024,768]{1,0:T(8,128)(2,1)}, f32[1024,128]{1,0:T(8,128)}) custom-call(bf16[1024,768]{1,0:T(8,128)(2,1)} %add_convert_fusion.2.q_ref, bf16[1024,768]{1,0:T(8,128)(2,1)} %convolution_convert_fusion.10.k_ref, bf16[1024,768]{1,0:T(8,128)(2,1)} %add_convert_fusion.1.v_ref, s32[1024,1]{1,0:T(8,128)} %copy.59.segq_ref, ...), custom_call_target="tpu_custom_call" | custom-call | flops 3221225472 | bytes 6291456 | tf_op jit(solution)/shard_map/pallas_call | solution.py:139
  136.4 11.3 %all-gather.8.cloned.1.call-done = bf16[64,96,768]{2,1,0:T(8,128)(2,1)} async-done(((bf16[2,96,768]{2,1,0:T(8,128)(2,1)}), bf16[64,96,768]{2,1,0:T(8,128)(2,1)}) %all-gather.8.cloned.1.call-update) | async-done | bytes 9437200 | tf_op jit(solution)/shard_map/all_gather | solution.py:206
  147.7 4.8 %fusion.59 = (bf16[1,1,8,96,768]{4,3,0,1,2:T(8,128)(2,1)S(1)}, bf16[1,1,8,96,768]{4,3,0,1,2:T(8,128)(2,1)S(1)}, bf16[1,1,8,96,768]{4,3,0,1,2:T(8,128)(2,1)S(1)},...) fusion(bf16[2,4,8,96,768]{4,3,0,1,2:T(8,128)(2,1)} %bitcast.120), kind=kLoop, calls=%fused_computation.160 | loop fusion | bytes 18874368 | tf_op jit(solution)/shard_map/slice | solution.py:316
  152.6 4.0 multiply_convert_fusion.3
  156.5 3.9 multiply_convert_fusion.2
  161.9 3.9 multiply_convert_fusion.1
  167.3 3.9 multiply_convert_fusion
  172.9 2.8 fusion.66
  182.9 8.3 %fusion.8 = bf16[768,3072]{1,0:T(8,128)(2,1)S(1)} fusion(bf16[1024,768]{1,0:T(8,128)(2,1)S(1)} %convert_element_type.157, bf16[1024,768]{0,1:T(8,128)(2,1)} %copy-done.50, bf16[1024,768]{0,1:T(8,128)(2,1)} %copy-done.49, bf16[1024,768]{0,1:T(8,128)(2,1)} %copy-done.48, bf16[1024,768]{0,1:T(8,128)(2,1)S(1)} %copy-done.47), kind=kOutput, calls=%fused_computation.11 | convolution fusion | flops 4859363328 | bytes 12582912 | tf_op jit(solution)/shard_map/dot_general | solution.py:21
  191.2 4.8 %fusion.23 = bf16[1024,768]{0,1:T(8,128)(2,1)S(1)} fusion(f32[1024,768]{0,1:T(8,128)} %get-tuple-element.168, f32[768]{0:T(1024)S(1)} %get-tuple-element.118, bf16[1024,768]{1,0:T(8,128)(2,1)S(1)} %convert_element_type.157, bf16[768,768]{1,0:T(8,128)(2,1)S(1)} %bitcast.147), kind=kOutput, calls=%fused_computation.35 | convolution fusion | flops 1224474624 | bytes 7474176 | tf_op jit(solution)/shard_map/dot_general | solution.py:27
  196.1 3.5 fusion.30
  199.6 3.2 fusion.37
  202.9 3.3 fusion.44
  206.2 3.1 fusion.67
  209.3 3.1 fusion.68
  212.4 3.1 fusion.69
  215.5 15.0 %convolution_convert_fusion = bf16[768,3072]{1,0:T(8,128)(2,1)S(1)} fusion(bf16[1024,768]{1,0:T(8,128)(2,1)} %fusion.46, bf16[1024,768]{0,1:T(8,128)(2,1)S(1)} %fusion.44, bf16[1024,768]{0,1:T(8,128)(2,1)S(1)} %fusion.37, bf16[1024,768]{0,1:T(8,128)(2,1)S(1)} %fusion.30, bf16[1024,768]{0,1:T(8,128)(2,1)S(1)} %fusion.23), kind=kOutput, calls=%fused_computation.10 | convolution fusion | flops 4859363328 | bytes 12582912 | tf_op jit(solution)/shard_map/dot_general | solution.py:21
  239.9 8.7 %add_add_fusion.1 = f32[1024,768]{1,0:T(8,128)} fusion(f32[1024,768]{1,0:T(8,128)} %fusion.69, f32[1024,768]{1,0:T(8,128)} %fusion.68, f32[1024,768]{1,0:T(8,128)} %copy-done.2, f32[1024,768]{1,0:T(8,128)} %fusion.67, bf16[1024,768]{0,1:T(8,128)(2,1)} %copy-done.7, bf16[768,768]{1,0:T(8,128)(2,1)} %bitcast.122), kind=kOutput, calls=%fused_computation.62 | convolution fusion | flops 1211105280 | bytes 18481152 | tf_op jit(solution)/shard_map/dot_general | solution.py:27
  248.7 3.1 multiply_reduce_fusion
  253.4 2.6 convolution_convert_fusion.1.dctx_ref
  256.0 2.5 convolution_convert_fusion.11.out_t_ref
  258.6 69.0 %shard_map.306 = (bf16[1024,768]{1,0:T(8,128)(2,1)}, bf16[1024,768]{1,0:T(8,128)(2,1)}, bf16[1024,768]{1,0:T(8,128)(2,1)}, bf16[768,3072]{1,0:T(8,128)(2,1)}, f32[8,768]{1,0:T(8,128)}) custom-call(bf16[1024,768]{1,0:T(8,128)(2,1)} %add_convert_fusion.2.q_ref, bf16[1024,768]{1,0:T(8,128)(2,1)} %convolution_convert_fusion.10.k_ref, ...), custom_call_target="tpu_custom_call" | custom-call | flops 11676942336 | bytes 16908288 | tf_op jit(solution)/shard_map/pallas_call | solution.py:163
  329.4 3.9 convert_reduce_fusion
  334.3 39.2 %psum.7 = f32[9216]{0:T(1024)S(1)} all-reduce(f32[9216]{0:T(1024)S(1)} %constant_dynamic-update-slice_fusion.5), channel_id=1, replica_groups=mesh['dp'=8,'tensor'=4] {'dp','tensor'}, use_global_device_ids=true, to_apply=%region_17.18 | all-reduce | flops 9216 | bytes 73728 | tf_op jit(solution)/shard_map/psum | solution.py:358
  374.9 3.3 fusion.70
  381.0 3.1 add_add_fusion
  388.5 36.8 %reduce-scatter.8.cloned.1.call-done = bf16[96,1,2304]{2,0,1:T(8,128)(2,1)} async-done(((bf16[96,4,2304]{2,0,1:T(8,128)(2,1)}), bf16[96,1,2304]{2,0,1:T(8,128)(2,1)}) %reduce-scatter.8.cloned.1.call-update) | async-done | bytes 442384 | tf_op jit(solution)/shard_map/reduce_scatter | solution.py:235
  (190 shorter events, 58.2 us)
Async XLA Ops:
  7.2 69.7 %copy-start = (s32[4,1024]{1,0:T(4,128)S(1)}, s32[4,1024]{1,0:T(4,128)}, u32[]{:S(2)}) copy-start(s32[4,1024]{1,0:T(4,128)} %param.19) | copy-start | bytes 49156
  7.2 56.2 %copy-start.39 = (f32[192]{0:T(256)S(1)}, f32[192]{0:T(256)}, u32[]{:S(2)}) copy-start(f32[192]{0:T(256)} %param.21) | copy-start | bytes 2308
  7.2 56.2 %copy-start.40 = (f32[192]{0:T(256)S(1)}, f32[192]{0:T(256)}, u32[]{:S(2)}) copy-start(f32[192]{0:T(256)} %param.24) | copy-start | bytes 2308
  7.2 56.2 %copy-start.38 = (f32[768]{0:T(1024)S(1)}, f32[768]{0:T(1024)}, u32[]{:S(2)}) copy-start(f32[768]{0:T(1024)} %param.30) | copy-start | bytes 9220
  7.3 56.2 %all-gather.6.cloned.1.call-start = ((), (), s32[]{:S(2)}) async-start(), calls=%async_computation.3 | async-start | bytes 2949120 | tf_op jit(solution)/shard_map/all_gather | solution.py:193
  9.6 138.1 %all-gather.8.cloned.1.call-start = ((), (), s32[]{:S(2)}) async-start(), calls=%async_computation.7 | async-start | bytes 9732096 | tf_op jit(solution)/shard_map/all_gather | solution.py:206
  10.5 317.1 %reduce-scatter.4.cloned.1.call-start = ((), (), s32[]{:S(2)}) async-start(), calls=%async_computation.4 | async-start | bytes 10616832 | tf_op jit(solution)/shard_map/reduce_scatter | solution.py:217
  63.5 16.8 %collective-permute-start = (bf16[4,2,192,768]{3,2,1,0:T(8,128)(2,1)}, bf16[4,2,192,768]{3,2,1,0:T(8,128)(2,1)}, u32[]{:S(2)}, u32[]{:S(2)}) collective-permute-start(bf16[4,2,192,768]{3,2,1,0:T(8,128)(2,1)} %all-gather.6.cloned.1.call-done), channel_id=1, source_target_pairs={{0,4},{4,0},{8,12},{12,8},{16,20},{20,16},{24,28},{28,24},{1,5},{5... | collective-permute-start | bytes 7077896 | tf_op jit(solution)/shard_map/ppermute | solution.py:196
  80.2 9.5 %copy-start.9 = (bf16[1024,768]{1,0:T(8,128)(2,1)}, bf16[1024,768]{1,0:T(8,128)(2,1)S(1)}, u32[]{:S(2)}) copy-start(bf16[1024,768]{1,0:T(8,128)(2,1)S(1)} %constant_dynamic-slice_fusion.2.x_ref.xall_ref) | copy-start | bytes 4718596
  82.8 48.3 %copy-start.4 = (bf16[4,2,192,768]{3,2,1,0:T(8,128)(2,1)}, bf16[4,2,192,768]{3,2,1,0:T(8,128)(2,1)S(1)}, u32[]{:S(2)}) copy-start(bf16[4,2,192,768]{3,2,1,0:T(8,128)(2,1)S(1)} %get-tuple-element.134) | copy-start | bytes 7077892
  84.4 5.3 %copy-start.25 = (bf16[4,1,192,768]{3,2,1,0:T(8,128)(2,1)}, bf16[4,1,192,768]{3,2,1,0:T(8,128)(2,1)S(1)}, u32[]{:S(2)}) copy-start(bf16[4,1,192,768]{3,2,1,0:T(8,128)(2,1)S(1)} %get-tuple-element.171) | copy-start | bytes 3538948
  127.5 3.6 copy-start.14
  127.5 4.1 copy-start.10
  127.5 4.1 copy-start.36
  147.7 4.8 %copy-start.22 = (bf16[1024,768]{1,0:T(8,128)(2,1)S(1)}, bf16[1024,768]{1,0:T(8,128)(2,1)}, u32[]{:S(2)}) copy-start(bf16[1024,768]{1,0:T(8,128)(2,1)} %fusion.46) | copy-start | bytes 4718596
  152.5 4.0 copy-start.27
  152.5 14.7 %copy-start.11 = (bf16[1,1,8,96,768]{4,3,0,1,2:T(8,128)(2,1)}, bf16[1,1,8,96,768]{4,3,0,1,2:T(8,128)(2,1)S(1)}, u32[]{:S(2)}) copy-start(bf16[1,1,8,96,768]{4,3,0,1,2:T(8,128)(2,1)S(1)} %get-tuple-element.128) | copy-start | bytes 3538948
  152.5 18.6 %copy-start.29 = (bf16[1,1,8,96,768]{4,3,0,1,2:T(8,128)(2,1)}, bf16[1,1,8,96,768]{4,3,0,1,2:T(8,128)(2,1)S(1)}, u32[]{:S(2)}) copy-start(bf16[1,1,8,96,768]{4,3,0,1,2:T(8,128)(2,1)S(1)} %get-tuple-element.127) | copy-start | bytes 3538948
  156.5 16.3 %copy-start.46 = (bf16[1024,768]{0,1:T(8,128)(2,1)}, bf16[1024,768]{0,1:T(8,128)(2,1)S(1)}, u32[]{:S(2)}) copy-start(bf16[1024,768]{0,1:T(8,128)(2,1)S(1)} %get-tuple-element.167) | copy-start | bytes 4718596
  172.8 3.3 slice-start
  172.9 3.3 slice-start.1
  191.2 4.8 %copy-start.45 = (f32[1024,768]{0,1:T(8,128)S(1)}, f32[1024,768]{0,1:T(8,128)}, u32[]{:S(2)}) copy-start(f32[1024,768]{0,1:T(8,128)} %get-tuple-element.166) | copy-start | bytes 9437188
  196.0 19.5 %copy-start.18 = (bf16[1024,768]{0,1:T(8,128)(2,1)}, bf16[1024,768]{0,1:T(8,128)(2,1)S(1)}, u32[]{:S(2)}) copy-start(bf16[1024,768]{0,1:T(8,128)(2,1)S(1)} %fusion.23) | copy-start | bytes 4718596
  196.0 3.5 copy-start.43
  199.5 16.0 %copy-start.20 = (bf16[1024,768]{0,1:T(8,128)(2,1)}, bf16[1024,768]{0,1:T(8,128)(2,1)S(1)}, u32[]{:S(2)}) copy-start(bf16[1024,768]{0,1:T(8,128)(2,1)S(1)} %fusion.30) | copy-start | bytes 4718596
  202.8 12.7 %copy-start.21 = (bf16[1024,768]{0,1:T(8,128)(2,1)}, bf16[1024,768]{0,1:T(8,128)(2,1)S(1)}, u32[]{:S(2)}) copy-start(bf16[1024,768]{0,1:T(8,128)(2,1)S(1)} %fusion.37) | copy-start | bytes 4718596
  206.1 9.4 %copy-start.7 = (bf16[1024,768]{0,1:T(8,128)(2,1)}, bf16[1024,768]{0,1:T(8,128)(2,1)S(1)}, u32[]{:S(2)}) copy-start(bf16[1024,768]{0,1:T(8,128)(2,1)S(1)} %fusion.44) | copy-start | bytes 4718596
  248.6 135.4 %reduce-scatter.6.cloned.1.call-start = ((), (), s32[]{:S(2)}) async-start(), calls=%async_computation.5 | async-start | bytes 5308416 | tf_op jit(solution)/shard_map/reduce_scatter | solution.py:217
  327.6 97.7 %reduce-scatter.8.cloned.1.call-start = ((), (), s32[]{:S(2)}) async-start(), calls=%async_computation.6 | async-start | bytes 2211840 | tf_op jit(solution)/shard_map/reduce_scatter | solution.py:235
  374.9 3.3 copy-start.24
  374.9 3.3 copy-start.42
  385.2 44.5 %copy-start.1 = (s32[4,1024]{1,0:T(4,128)S(1)}, s32[4,1024]{1,0:T(4,128)}, u32[]{:S(2)}) copy-start(s32[4,1024]{1,0:T(4,128)} %param.19) | copy-start | bytes 49156
  (27 other events, 57.4 us)
Sparse Core Ops, SparseCore 0:
  10.2 53.1 all-gather.5
  66.8 80.8 all-gather.7
  248.8 75.0 reduce-scatter.3
  327.7 53.4 reduce-scatter.5
  386.7 38.5 reduce-scatter.7

commit v3 on v2

--- a/solution.py
+++ b/solution.py
@@ -336,8 +336,10 @@
     hidden_low = jnp.concatenate(hidden_parts, axis=1)
     grad_up_bias = jnp.sum(grad_pre, 0, dtype=jnp.float32)
     ffn_grads = [contract_rows(first_low, grad_pre), contract_rows(down_low, hidden_low)]
-    ffn_joined, first_grad = lax.optimization_barrier((part_major(ffn_grads), first_grad))
-    ffn_rows = scatter_rows([ffn_joined])
+    ffn_joined, first_grad = lax.optimization_barrier(
+        (jnp.stack([grad.astype(jnp.bfloat16) for grad in ffn_grads]), first_grad)
+    )
+    ffn_rows = lax.psum_scatter(ffn_joined, "dp", scatter_dimension=1, tiled=True)
     grad_first_gain = jnp.sum(first_grad * first_unit, 0)
     grad_first_shift = jnp.sum(first_grad, 0)
     attn_grad = normalize_back(first_grad, first_unit, first_inv, first_gain)
@@ -382,6 +384,9 @@
     )
     attn_rows, small, input_grad = lax.optimization_barrier((attn_rows, small, input_grad))
     ffn_width = up_weight.shape[1]
+    grads_count, ffn_rows_count, _ = ffn_rows.shape
+    ffn_rows = ffn_rows.reshape(grads_count, ffn_rows_count, part_count, -1).transpose(1, 2, 0, 3)
+    ffn_rows = ffn_rows.reshape(ffn_rows_count, -1)
     summed = scatter_parts([ffn_rows, attn_rows], [[ffn_width] * 2, [head_width] * 4])
     split_width = 2 * head_width * part_count + up_bias.shape[0] * part_count
     split = small[:split_width]

time: 441 us -> 444 us (level)
  other arithmetic: 25.5 us -> 33.7 us
  local copies, waits for them, and re-layouts: 31.8 us -> 25.6 us
    another operation x0 -> x1, other arithmetic: none -> 8.29 us  [on_device(): jnp.stack([grad.astype(jnp.bfloat16) for grad in ffn_grads])]
    unnamed x124 -> x111, local copies, waits for them, and re-layouts: 15.5 us -> 7.21 us
  transfers between devices with their start and end apart: 6 -> 6, of which waited for: 3 -> 3; matrix products, arithmetic and copies ran while one was open for 11% -> 12% of each run, Pallas kernels for 24% -> 24%
where the time goes in v3:
time: 444 us; the launch traced here: 440 us
  matrix products  107 us (24%)
  Pallas kernels  104 us (23%)
  waiting for transfers between devices  101 us (23%)
  blocking collectives  52.8 us (12%)
  other arithmetic  33.7 us (8%)
  local copies, waits for them, and re-layouts  25.6 us (6%)
  between operations  14.9 us (3%)
    pallas_call x1, Pallas kernels, attention_backward(): pl.pallas_call(functools.partial(attn_bwd_kernel, parts), out_shape=tuple...  69 us
    all_gather x1, waiting for transfers between devices, gather_shards(): gathered = lax.all_gather(mine, 'tensor', axis=0, tiled=False)  52.9 us
    dot_general x12, matrix products, contract_last(): lax.dot_general(left_side, right_side, (((1,), (1,)), ((), ())), preferre...  43.2 us
    psum x1, blocking collectives, on_device(): lax.psum(jnp.concatenate([grad_query_bias, grad_value_bias, grad_up_bias,...  39.7 us
    dot_general x15, matrix products, product(): return jnp.dot(left_side, right_side, preferred_element_type=jnp.float32)  36.9 us
    reduce_scatter x1, waiting for transfers between devices, scatter_parts(): lax.psum_scatter(joined, 'tensor', scatter_dimension=1, tiled=True)[:, 0]  36.8 us
    pallas_call x1, Pallas kernels, attention_forward(): pl.pallas_call(attn_fwd_kernel, out_shape=(jax.ShapeDtypeStruct((length,...  35.2 us
    dot_general x3, matrix products, contract_rows(): lax.dot_general(left_side, right_side, (((0,), (0,)), ((), ())), preferre...  27 us
  transfers between devices with their start and end apart: 6, of which 3 were waited for; matrix products, arithmetic and copies ran while one was open for 12% of the time, Pallas kernels for 24%

profile of v3, /device:TPU:0, one launch (start us, length us, event | category | flops | bytes accessed | tf_op | source)
XLA Modules:
  0.0 439.8 jit_solution(13190988112920347088)
XLA Ops:
  10.5 52.9 %all-gather.6.cloned.1.call-done = bf16[4,2,192,768]{3,2,1,0:T(8,128)(2,1)} async-done(((bf16[1,2,192,768]{3,2,1,0:T(8,128)(2,1)}), bf16[4,2,192,768]{3,2,1,0:T(8,128)(2,1)}) %all-gather.6.cloned.1.call-update) | async-done | bytes 2359312 | tf_op jit(solution)/shard_map/all_gather | solution.py:193
  63.6 13.1 %all-gather.2 = f32[4,1,1152]{2,1,0:T(1,128)S(1)} all-gather(f32[1,1,1152]{2,1,0:T(1,128)S(1)} %reshape.201), channel_id=2, replica_groups=mesh['dp'=8,'tensor'=4] {'tensor'}, dimensions={0}, use_global_device_ids=true | all-gather | bytes 23040 | tf_op jit(solution)/shard_map/all_gather | solution.py:278
  87.0 2.6 add_convert_fusion.1.v_ref
  89.6 2.6 add_convert_fusion.2.q_ref
  92.2 35.2 %shard_map.305 = (bf16[1024,768]{1,0:T(8,128)(2,1)}, f32[1024,128]{1,0:T(8,128)}) custom-call(bf16[1024,768]{1,0:T(8,128)(2,1)} %add_convert_fusion.2.q_ref, bf16[1024,768]{1,0:T(8,128)(2,1)} %convolution_convert_fusion.10.k_ref, bf16[1024,768]{1,0:T(8,128)(2,1)} %add_convert_fusion.1.v_ref, s32[1024,1]{1,0:T(8,128)} %copy.59.segq_ref, ...), custom_call_target="tpu_custom_call" | custom-call | flops 3221225472 | bytes 6291456 | tf_op jit(solution)/shard_map/pallas_call | solution.py:139
  136.2 11.5 %all-gather.8.cloned.1.call-done = bf16[64,96,768]{2,1,0:T(8,128)(2,1)} async-done(((bf16[2,96,768]{2,1,0:T(8,128)(2,1)}), bf16[64,96,768]{2,1,0:T(8,128)(2,1)}) %all-gather.8.cloned.1.call-update) | async-done | bytes 9437200 | tf_op jit(solution)/shard_map/all_gather | solution.py:206
  147.7 4.5 %fusion.63 = (bf16[1,1,8,96,768]{4,3,0,1,2:T(8,128)(2,1)S(1)}, bf16[1,1,8,96,768]{4,3,0,1,2:T(8,128)(2,1)S(1)}, bf16[1,1,8,96,768]{4,3,0,1,2:T(8,128)(2,1)S(1)},...) fusion(bf16[2,4,8,96,768]{4,3,0,1,2:T(8,128)(2,1)} %bitcast.123), kind=kLoop, calls=%fused_computation.154 | loop fusion | bytes 18874368 | tf_op jit(solution)/shard_map/slice | solution.py:316
  152.2 3.9 multiply_convert_fusion.3
  156.1 3.9 multiply_convert_fusion.2
  161.5 3.8 multiply_convert_fusion.1
  166.8 3.9 multiply_convert_fusion
  172.6 2.7 fusion.70
  182.6 9.6 %fusion.11 = bf16[1,768,3072]{2,1,0:T(8,128)(2,1)} fusion(bf16[1024,768]{1,0:T(8,128)(2,1)S(1)} %convert_element_type.155, bf16[1024,768]{0,1:T(8,128)(2,1)} %copy-done.47, bf16[1024,768]{0,1:T(8,128)(2,1)} %copy-done.46, bf16[1024,768]{0,1:T(8,128)(2,1)S(1)} %copy-done.45, bf16[1024,768]{0,1:T(8,128)(2,1)S(1)} %get-tuple-element.167), kind=kOutput, calls=%fused_computation.24 | convolution fusion | flops 4859363328 | bytes 12582912 | tf_op jit(solution)/shard_map/dot_general | solution.py:21
  192.2 4.8 %fusion.27 = bf16[1024,768]{0,1:T(8,128)(2,1)S(1)} fusion(f32[1024,768]{0,1:T(8,128)} %get-tuple-element.168, f32[768]{0:T(1024)S(1)} %get-tuple-element.118, bf16[1024,768]{1,0:T(8,128)(2,1)S(1)} %convert_element_type.155, bf16[768,768]{1,0:T(8,128)(2,1)S(1)} %bitcast.150), kind=kOutput, calls=%fused_computation.38 | convolution fusion | flops 1224474624 | bytes 7474176 | tf_op jit(solution)/shard_map/dot_general | solution.py:27
  197.0 3.4 fusion.34
  200.5 3.2 fusion.41
  203.7 3.2 fusion.48
  207.0 3.2 fusion.71
  210.2 3.1 fusion.72
  213.3 3.1 fusion.73
  216.5 14.9 %fusion.14 = bf16[1,768,3072]{2,1,0:T(8,128)(2,1)} fusion(bf16[1024,768]{1,0:T(8,128)(2,1)S(1)} %copy-done.21, bf16[1024,768]{0,1:T(8,128)(2,1)S(1)} %fusion.48, bf16[1024,768]{0,1:T(8,128)(2,1)S(1)} %fusion.41, bf16[1024,768]{0,1:T(8,128)(2,1)S(1)} %fusion.34, bf16[1024,768]{0,1:T(8,128)(2,1)S(1)} %fusion.27), kind=kOutput, calls=%fused_computation.25 | convolution fusion | flops 4859363328 | bytes 12582912 | tf_op jit(solution)/shard_map/dot_general | solution.py:21
  231.4 8.3 %pad_maximum_fusion = bf16[2,768,3072]{2,1,0:T(8,128)(2,1)} fusion(bf16[1,768,3072]{2,1,0:T(8,128)(2,1)} %fusion.11, bf16[1,768,3072]{2,1,0:T(8,128)(2,1)} %fusion.14), kind=kLoop, calls=%fused_computation.1 | loop fusion | flops 4718592 | bytes 18874368 | tf_op jit(solution)/shard_map/stack | solution.py:340
  239.7 8.7 %add_add_fusion.1 = f32[1024,768]{1,0:T(8,128)} fusion(f32[1024,768]{1,0:T(8,128)} %fusion.73, f32[1024,768]{1,0:T(8,128)} %fusion.72, f32[1024,768]{1,0:T(8,128)} %copy-done.2, f32[1024,768]{1,0:T(8,128)} %fusion.71, bf16[1024,768]{0,1:T(8,128)(2,1)} %copy-done.7, bf16[768,768]{1,0:T(8,128)(2,1)} %bitcast.125), kind=kOutput, calls=%fused_computation.65 | convolution fusion | flops 1211105280 | bytes 18481152 | tf_op jit(solution)/shard_map/dot_general | solution.py:27
  248.5 3.1 multiply_reduce_fusion
  253.3 2.6 convolution_convert_fusion.1.dctx_ref
  258.4 69.0 %shard_map.306 = (bf16[1024,768]{1,0:T(8,128)(2,1)}, bf16[1024,768]{1,0:T(8,128)(2,1)}, bf16[1024,768]{1,0:T(8,128)(2,1)}, bf16[768,3072]{1,0:T(8,128)(2,1)}, f32[8,768]{1,0:T(8,128)}) custom-call(bf16[1024,768]{1,0:T(8,128)(2,1)} %add_convert_fusion.2.q_ref, bf16[1024,768]{1,0:T(8,128)(2,1)} %convolution_convert_fusion.10.k_ref, ...), custom_call_target="tpu_custom_call" | custom-call | flops 11676942336 | bytes 16908288 | tf_op jit(solution)/shard_map/pallas_call | solution.py:163
  329.2 3.9 convert_reduce_fusion
  334.1 39.7 %psum.7 = f32[9216]{0:T(1024)} all-reduce(f32[9216]{0:T(1024)S(1)} %constant_dynamic-update-slice_fusion), channel_id=1, replica_groups=mesh['dp'=8,'tensor'=4] {'dp','tensor'}, use_global_device_ids=true, to_apply=%region_17.18 | all-reduce | flops 9216 | bytes 73728 | tf_op jit(solution)/shard_map/psum | solution.py:360
  373.8 2.8 reshape.197
  378.6 3.0 fusion.74
  384.4 3.1 add_add_fusion
  391.9 36.8 %reduce-scatter.8.cloned.1.call-done = bf16[96,1,2304]{2,0,1:T(8,128)(2,1)} async-done(((bf16[96,4,2304]{2,0,1:T(8,128)(2,1)}), bf16[96,1,2304]{2,0,1:T(8,128)(2,1)}) %reduce-scatter.8.cloned.1.call-update) | async-done | bytes 442384 | tf_op jit(solution)/shard_map/reduce_scatter | solution.py:235
  (179 shorter events, 54.7 us)
Async XLA Ops:
  7.2 69.7 %copy-start = (s32[4,1024]{1,0:T(4,128)S(1)}, s32[4,1024]{1,0:T(4,128)}, u32[]{:S(2)}) copy-start(s32[4,1024]{1,0:T(4,128)} %param.19) | copy-start | bytes 49156
  7.2 56.2 %copy-start.37 = (f32[192]{0:T(256)S(1)}, f32[192]{0:T(256)}, u32[]{:S(2)}) copy-start(f32[192]{0:T(256)} %param.21) | copy-start | bytes 2308
  7.2 56.2 %copy-start.38 = (f32[192]{0:T(256)S(1)}, f32[192]{0:T(256)}, u32[]{:S(2)}) copy-start(f32[192]{0:T(256)} %param.24) | copy-start | bytes 2308
  7.2 56.2 %copy-start.36 = (f32[768]{0:T(1024)S(1)}, f32[768]{0:T(1024)}, u32[]{:S(2)}) copy-start(f32[768]{0:T(1024)} %param.30) | copy-start | bytes 9220
  7.3 56.2 %all-gather.6.cloned.1.call-start = ((), (), s32[]{:S(2)}) async-start(), calls=%async_computation.3 | async-start | bytes 2949120 | tf_op jit(solution)/shard_map/all_gather | solution.py:193
  9.6 138.1 %all-gather.8.cloned.1.call-start = ((), (), s32[]{:S(2)}) async-start(), calls=%async_computation.7 | async-start | bytes 9732096 | tf_op jit(solution)/shard_map/all_gather | solution.py:206
  10.5 316.9 %reduce-scatter.4.cloned.1.call-start = ((), (), s32[]{:S(2)}) async-start(), calls=%async_computation.4 | async-start | bytes 10616832 | tf_op jit(solution)/shard_map/reduce_scatter | solution.py:342
  63.5 16.8 %collective-permute-start = (bf16[4,2,192,768]{3,2,1,0:T(8,128)(2,1)}, bf16[4,2,192,768]{3,2,1,0:T(8,128)(2,1)}, u32[]{:S(2)}, u32[]{:S(2)}) collective-permute-start(bf16[4,2,192,768]{3,2,1,0:T(8,128)(2,1)} %all-gather.6.cloned.1.call-done), channel_id=1, source_target_pairs={{0,4},{4,0},{8,12},{12,8},{16,20},{20,16},{24,28},{28,24},{1,5},{5... | collective-permute-start | bytes 7077896 | tf_op jit(solution)/shard_map/ppermute | solution.py:196
  80.2 9.4 %copy-start.9 = (bf16[1024,768]{1,0:T(8,128)(2,1)}, bf16[1024,768]{1,0:T(8,128)(2,1)S(1)}, u32[]{:S(2)}) copy-start(bf16[1024,768]{1,0:T(8,128)(2,1)S(1)} %constant_dynamic-slice_fusion.2.x_ref.xall_ref) | copy-start | bytes 4718596
  82.8 48.1 %copy-start.4 = (bf16[4,2,192,768]{3,2,1,0:T(8,128)(2,1)}, bf16[4,2,192,768]{3,2,1,0:T(8,128)(2,1)S(1)}, u32[]{:S(2)}) copy-start(bf16[4,2,192,768]{3,2,1,0:T(8,128)(2,1)S(1)} %get-tuple-element.134) | copy-start | bytes 7077892
  84.4 5.2 %copy-start.25 = (bf16[4,1,192,768]{3,2,1,0:T(8,128)(2,1)}, bf16[4,1,192,768]{3,2,1,0:T(8,128)(2,1)S(1)}, u32[]{:S(2)}) copy-start(bf16[4,1,192,768]{3,2,1,0:T(8,128)(2,1)S(1)} %get-tuple-element.171) | copy-start | bytes 3538948
  127.3 3.6 copy-start.14
  127.3 4.1 copy-start.10
  127.3 4.1 copy-start.34
  147.7 4.5 %copy-start.21 = (bf16[1024,768]{1,0:T(8,128)(2,1)S(1)}, bf16[1024,768]{1,0:T(8,128)(2,1)}, u32[]{:S(2)}) copy-start(bf16[1024,768]{1,0:T(8,128)(2,1)} %fusion.50) | copy-start | bytes 4718596
  152.2 14.6 %copy-start.11 = (bf16[1,1,8,96,768]{4,3,0,1,2:T(8,128)(2,1)}, bf16[1,1,8,96,768]{4,3,0,1,2:T(8,128)(2,1)S(1)}, u32[]{:S(2)}) copy-start(bf16[1,1,8,96,768]{4,3,0,1,2:T(8,128)(2,1)S(1)} %get-tuple-element.128) | copy-start | bytes 3538948
  172.6 3.3 slice-start
  172.6 3.3 slice-start.1
  192.2 4.8 %copy-start.43 = (f32[1024,768]{0,1:T(8,128)S(1)}, f32[1024,768]{0,1:T(8,128)}, u32[]{:S(2)}) copy-start(f32[1024,768]{0,1:T(8,128)} %get-tuple-element.166) | copy-start | bytes 9437188
  197.0 19.5 %copy-start.18 = (bf16[1024,768]{0,1:T(8,128)(2,1)}, bf16[1024,768]{0,1:T(8,128)(2,1)S(1)}, u32[]{:S(2)}) copy-start(bf16[1024,768]{0,1:T(8,128)(2,1)S(1)} %fusion.27) | copy-start | bytes 4718596
  197.0 3.5 copy-start.41
  200.4 16.0 %copy-start.20 = (bf16[1024,768]{0,1:T(8,128)(2,1)}, bf16[1024,768]{0,1:T(8,128)(2,1)S(1)}, u32[]{:S(2)}) copy-start(bf16[1024,768]{0,1:T(8,128)(2,1)S(1)} %fusion.34) | copy-start | bytes 4718596
  200.5 3.3 copy-start.42
  203.7 12.7 %copy-start.22 = (bf16[1024,768]{0,1:T(8,128)(2,1)}, bf16[1024,768]{0,1:T(8,128)(2,1)S(1)}, u32[]{:S(2)}) copy-start(bf16[1024,768]{0,1:T(8,128)(2,1)S(1)} %fusion.41) | copy-start | bytes 4718596
  207.0 9.5 %copy-start.7 = (bf16[1024,768]{0,1:T(8,128)(2,1)}, bf16[1024,768]{0,1:T(8,128)(2,1)S(1)}, u32[]{:S(2)}) copy-start(bf16[1024,768]{0,1:T(8,128)(2,1)S(1)} %fusion.48) | copy-start | bytes 4718596
  248.5 139.0 %reduce-scatter.6.cloned.1.call-start = ((), (), s32[]{:S(2)}) async-start(), calls=%async_computation.5 | async-start | bytes 5308416 | tf_op jit(solution)/shard_map/reduce_scatter | solution.py:217
  248.5 3.1 copy-start.3
  252.8 3.1 copy-start.5
  327.4 101.3 %reduce-scatter.8.cloned.1.call-start = ((), (), s32[]{:S(2)}) async-start(), calls=%async_computation.6 | async-start | bytes 2211840 | tf_op jit(solution)/shard_map/reduce_scatter | solution.py:235
  373.8 4.8 %copy-start.26 = (bf16[4,1,192,768]{3,2,1,0:T(8,128)(2,1)S(1)}, bf16[4,1,192,768]{3,2,1,0:T(8,128)(2,1)}, u32[]{:S(2)}) copy-start(bf16[4,1,192,768]{3,2,1,0:T(8,128)(2,1)} %copy-done.25) | copy-start | bytes 3538948
  378.6 3.0 copy-start.24
  388.6 44.5 %copy-start.1 = (s32[4,1024]{1,0:T(4,128)S(1)}, s32[4,1024]{1,0:T(4,128)}, u32[]{:S(2)}) copy-start(s32[4,1024]{1,0:T(4,128)} %param.19) | copy-start | bytes 49156
  (24 other events, 47.2 us)
Sparse Core Ops, SparseCore 0:
  10.2 53.1 all-gather.5
  66.8 80.8 all-gather.7
  248.6 75.0 reduce-scatter.3
  327.6 53.4 reduce-scatter.5
  390.1 38.5 reduce-scatter.7

commit v4 on v2

--- a/solution.py
+++ b/solution.py
@@ -329,9 +329,10 @@
     grad_pre_parts = []
     for member in range(part_count):
         grad_hidden = contract_last(down_low, d_sh[member])
-        grad_pre = pulls[member](grad_hidden)[0].astype(jnp.bfloat16)
-        grad_pre_parts.append(grad_pre)
-        first_grad = first_grad + contract_last(grad_pre, u_sh[member])
+        grad_pre_parts.append(pulls[member](grad_hidden)[0].astype(jnp.bfloat16))
+    grad_pre_parts = lax.optimization_barrier(grad_pre_parts)
+    for member in range(part_count):
+        first_grad = first_grad + contract_last(grad_pre_parts[member], u_sh[member])
     grad_pre = jnp.concatenate(grad_pre_parts, axis=1)
     hidden_low = jnp.concatenate(hidden_parts, axis=1)
     grad_up_bias = jnp.sum(grad_pre, 0, dtype=jnp.float32)

time: 441 us -> 431 us (0.977)
  matrix products: 106 us -> 97.2 us
    dot_general x3, matrix products: 25.8 us -> 16.6 us  [contract_rows(): lax.dot_general(left_side, right_side, (((0,), (0,)), ((), ())), preferre...]
    unnamed x124 -> x129, local copies, waits for them, and re-layouts: 15.5 us -> 13.3 us
  transfers between devices with their start and end apart: 6 -> 6, of which waited for: 3 -> 3; matrix products, arithmetic and copies ran while one was open for 11% -> 12% of each run, Pallas kernels for 24% -> 24%
where the time goes in v4:
time: 431 us; the launch traced here: 427 us
  Pallas kernels  104 us (24%)
  waiting for transfers between devices  101 us (23%)
  matrix products  97.2 us (23%)
  blocking collectives  53.3 us (12%)
  local copies, waits for them, and re-layouts  28.6 us (7%)
  other arithmetic  27.7 us (6%)
  between operations  15 us (3%)
    pallas_call x1, Pallas kernels, attention_backward(): pl.pallas_call(functools.partial(attn_bwd_kernel, parts), out_shape=tuple...  68.6 us
    all_gather x1, waiting for transfers between devices, gather_shards(): gathered = lax.all_gather(mine, 'tensor', axis=0, tiled=False)  52.9 us
    dot_general x12, matrix products, contract_last(): lax.dot_general(left_side, right_side, (((1,), (1,)), ((), ())), preferre...  44 us
    psum x1, blocking collectives, on_device(): lax.psum(jnp.concatenate([grad_query_bias, grad_value_bias, grad_up_bias,...  40.1 us
    reduce_scatter x1, waiting for transfers between devices, scatter_parts(): lax.psum_scatter(joined, 'tensor', scatter_dimension=1, tiled=True)[:, 0]  36.9 us
    dot_general x15, matrix products, product(): return jnp.dot(left_side, right_side, preferred_element_type=jnp.float32)  36.5 us
    pallas_call x1, Pallas kernels, attention_forward(): pl.pallas_call(attn_fwd_kernel, out_shape=(jax.ShapeDtypeStruct((length,...  35.2 us
    dot_general x3, matrix products, contract_rows(): lax.dot_general(left_side, right_side, (((0,), (0,)), ((), ())), preferre...  16.6 us
  transfers between devices with their start and end apart: 6, of which 3 were waited for; matrix products, arithmetic and copies ran while one was open for 12% of the time, Pallas kernels for 24%

profile of v4, /device:TPU:0, one launch (start us, length us, event | category | flops | bytes accessed | tf_op | source)
XLA Modules:
  0.0 427.0 jit_solution(18318194625052910856)
XLA Ops:
  10.5 52.9 %all-gather.6.cloned.1.call-done = bf16[4,2,192,768]{3,2,1,0:T(8,128)(2,1)} async-done(((bf16[1,2,192,768]{3,2,1,0:T(8,128)(2,1)}), bf16[4,2,192,768]{3,2,1,0:T(8,128)(2,1)}) %all-gather.6.cloned.1.call-update) | async-done | bytes 2359312 | tf_op jit(solution)/shard_map/all_gather | solution.py:193
  63.6 13.1 %all-gather.2 = f32[4,1,1152]{2,1,0:T(1,128)S(1)} all-gather(f32[1,1,1152]{2,1,0:T(1,128)S(1)} %reshape.201), channel_id=2, replica_groups=mesh['dp'=8,'tensor'=4] {'tensor'}, dimensions={0}, use_global_device_ids=true | all-gather | bytes 23040 | tf_op jit(solution)/shard_map/all_gather | solution.py:278
  84.4 2.7 convolution_convert_fusion.10.k_ref
  87.1 2.6 add_convert_fusion.1.v_ref
  89.7 2.6 add_convert_fusion.2.q_ref
  92.3 35.2 %shard_map.305 = (bf16[1024,768]{1,0:T(8,128)(2,1)}, f32[1024,128]{1,0:T(8,128)}) custom-call(bf16[1024,768]{1,0:T(8,128)(2,1)} %add_convert_fusion.2.q_ref, bf16[1024,768]{1,0:T(8,128)(2,1)} %convolution_convert_fusion.10.k_ref, bf16[1024,768]{1,0:T(8,128)(2,1)} %add_convert_fusion.1.v_ref, s32[1024,1]{1,0:T(8,128)} %copy.75.segq_ref, ...), custom_call_target="tpu_custom_call" | custom-call | flops 3221225472 | bytes 6291456 | tf_op jit(solution)/shard_map/pallas_call | solution.py:139
  136.5 11.3 %all-gather.8.cloned.1.call-done = bf16[64,96,768]{2,1,0:T(8,128)(2,1)} async-done(((bf16[2,96,768]{2,1,0:T(8,128)(2,1)}), bf16[64,96,768]{2,1,0:T(8,128)(2,1)}) %all-gather.8.cloned.1.call-update) | async-done | bytes 9437200 | tf_op jit(solution)/shard_map/all_gather | solution.py:206
  147.7 4.8 %fusion.58 = (bf16[1,1,8,96,768]{4,3,0,1,2:T(8,128)(2,1)S(1)}, bf16[1,1,8,96,768]{4,3,0,1,2:T(8,128)(2,1)S(1)}, bf16[1,1,8,96,768]{4,3,0,1,2:T(8,128)(2,1)S(1)},...) fusion(bf16[2,4,8,96,768]{4,3,0,1,2:T(8,128)(2,1)} %bitcast.121), kind=kLoop, calls=%fused_computation.162 | loop fusion | bytes 18874368 | tf_op jit(solution)/shard_map/slice | solution.py:316
  152.5 3.8 multiply_convert_fusion.3
  156.4 3.9 multiply_convert_fusion.2
  161.7 3.9 multiply_convert_fusion.1
  167.1 3.9 multiply_convert_fusion
  172.7 2.6 fusion.65
  178.4 2.9 fusion.55
  183.0 8.7 %fusion.8 = bf16[768,3072]{1,0:T(8,128)(2,1)S(1)} fusion(bf16[1024,768]{1,0:T(8,128)(2,1)S(1)} %convert_element_type.157, bf16[1024,768]{0,1:T(8,128)(2,1)} %copy-done.51, bf16[1024,768]{0,1:T(8,128)(2,1)} %copy-done.50, bf16[1024,768]{0,1:T(8,128)(2,1)} %copy-done.49, bf16[1024,768]{0,1:T(8,128)(2,1)} %copy-done.48), kind=kOutput, calls=%fused_computation.10 | convolution fusion | flops 4859363328 | bytes 12582912 | tf_op jit(solution)/shard_map/dot_general | solution.py:21
  191.8 5.3 %fusion.44 = bf16[1024,768]{0,1:T(8,128)(2,1)S(1)} fusion(f32[1024,768]{0,1:T(8,128)} %get-tuple-element.170, f32[768]{0:T(1024)S(1)} %get-tuple-element.127, bf16[1024,768]{1,0:T(8,128)(2,1)S(1)} %convert_element_type.157, bf16[768,768]{1,0:T(8,128)(2,1)} %bitcast.148), kind=kOutput, calls=%fused_computation.55 | convolution fusion | flops 1224474624 | bytes 7474176 | tf_op jit(solution)/shard_map/dot_general | solution.py:27
  197.1 3.7 fusion.37
  200.8 3.2 fusion.30
  204.1 3.2 fusion.23
  207.3 3.1 fusion.66
  210.6 3.2 fusion.67
  213.7 3.1 fusion.68
  217.3 5.3 %convolution_convert_fusion = bf16[768,3072]{1,0:T(8,128)(2,1)S(1)} fusion(bf16[1024,768]{1,0:T(8,128)(2,1)S(1)} %copy-done.18, bf16[1024,3072]{0,1:T(8,128)(2,1)S(1)} %constant_dynamic-update-slice_fusion), kind=kOutput, calls=%fused_computation.9 | convolution fusion | flops 4834197504 | bytes 12582912 | tf_op jit(solution)/shard_map/dot_general | solution.py:21
  232.0 8.7 %add_add_fusion.1 = f32[1024,768]{1,0:T(8,128)} fusion(f32[1024,768]{1,0:T(8,128)} %fusion.68, f32[1024,768]{1,0:T(8,128)} %fusion.67, f32[1024,768]{1,0:T(8,128)} %copy-done.2, f32[1024,768]{1,0:T(8,128)} %fusion.66, bf16[1024,768]{0,1:T(8,128)(2,1)} %copy-done.8, bf16[768,768]{1,0:T(8,128)(2,1)} %bitcast.123), kind=kOutput, calls=%fused_computation.61 | convolution fusion | flops 1211105280 | bytes 18481152 | tf_op jit(solution)/shard_map/dot_general | solution.py:27
  240.9 3.7 multiply_reduce_fusion
  246.3 2.6 convolution_convert_fusion.1.dctx_ref
  251.7 68.6 %shard_map.306 = (bf16[1024,768]{1,0:T(8,128)(2,1)}, bf16[1024,768]{1,0:T(8,128)(2,1)}, bf16[1024,768]{1,0:T(8,128)(2,1)}, bf16[768,3072]{1,0:T(8,128)(2,1)}, f32[8,768]{1,0:T(8,128)}) custom-call(bf16[1024,768]{1,0:T(8,128)(2,1)} %add_convert_fusion.2.q_ref, bf16[1024,768]{1,0:T(8,128)(2,1)} %convolution_convert_fusion.10.k_ref, ...), custom_call_target="tpu_custom_call" | custom-call | flops 11676942336 | bytes 16908288 | tf_op jit(solution)/shard_map/pallas_call | solution.py:163
  320.6 3.8 convert_reduce_fusion
  325.4 40.1 %psum.7 = f32[9216]{0:T(1024)} all-reduce(f32[9216]{0:T(1024)S(1)} %constant_dynamic-update-slice_fusion.9), channel_id=1, replica_groups=mesh['dp'=8,'tensor'=4] {'dp','tensor'}, use_global_device_ids=true, to_apply=%region_17.18 | all-reduce | flops 9216 | bytes 73728 | tf_op jit(solution)/shard_map/psum | solution.py:359
  365.7 2.9 fusion.69
  371.4 3.1 add_add_fusion
  379.0 36.9 %reduce-scatter.8.cloned.1.call-done = bf16[96,1,2304]{2,0,1:T(8,128)(2,1)} async-done(((bf16[96,4,2304]{2,0,1:T(8,128)(2,1)}), bf16[96,1,2304]{2,0,1:T(8,128)(2,1)}) %reduce-scatter.8.cloned.1.call-update) | async-done | bytes 442384 | tf_op jit(solution)/shard_map/reduce_scatter | solution.py:235
  (196 shorter events, 56.3 us)
Async XLA Ops:
  7.2 69.7 %copy-start = (s32[4,1024]{1,0:T(4,128)S(1)}, s32[4,1024]{1,0:T(4,128)}, u32[]{:S(2)}) copy-start(s32[4,1024]{1,0:T(4,128)} %param.19) | copy-start | bytes 49156
  7.2 56.2 %copy-start.40 = (f32[768]{0:T(1024)S(1)}, f32[768]{0:T(1024)}, u32[]{:S(2)}) copy-start(f32[768]{0:T(1024)} %param.30) | copy-start | bytes 9220
  7.2 56.2 %copy-start.42 = (f32[192]{0:T(256)S(1)}, f32[192]{0:T(256)}, u32[]{:S(2)}) copy-start(f32[192]{0:T(256)} %param.24) | copy-start | bytes 2308
  7.2 56.2 %copy-start.41 = (f32[192]{0:T(256)S(1)}, f32[192]{0:T(256)}, u32[]{:S(2)}) copy-start(f32[192]{0:T(256)} %param.21) | copy-start | bytes 2308
  7.3 56.2 %all-gather.6.cloned.1.call-start = ((), (), s32[]{:S(2)}) async-start(), calls=%async_computation.3 | async-start | bytes 2949120 | tf_op jit(solution)/shard_map/all_gather | solution.py:193
  9.6 138.1 %all-gather.8.cloned.1.call-start = ((), (), s32[]{:S(2)}) async-start(), calls=%async_computation.7 | async-start | bytes 9732096 | tf_op jit(solution)/shard_map/all_gather | solution.py:206
  10.5 309.9 %reduce-scatter.4.cloned.1.call-start = ((), (), s32[]{:S(2)}) async-start(), calls=%async_computation.4 | async-start | bytes 10616832 | tf_op jit(solution)/shard_map/reduce_scatter | solution.py:217
  63.5 16.8 %collective-permute-start = (bf16[4,2,192,768]{3,2,1,0:T(8,128)(2,1)}, bf16[4,2,192,768]{3,2,1,0:T(8,128)(2,1)}, u32[]{:S(2)}, u32[]{:S(2)}) collective-permute-start(bf16[4,2,192,768]{3,2,1,0:T(8,128)(2,1)} %all-gather.6.cloned.1.call-done), channel_id=1, source_target_pairs={{0,4},{4,0},{8,12},{12,8},{16,20},{20,16},{24,28},{28,24},{1,5},{5... | collective-permute-start | bytes 7077896 | tf_op jit(solution)/shard_map/ppermute | solution.py:196
  80.2 9.5 %copy-start.9 = (bf16[1024,768]{1,0:T(8,128)(2,1)}, bf16[1024,768]{1,0:T(8,128)(2,1)S(1)}, u32[]{:S(2)}) copy-start(bf16[1024,768]{1,0:T(8,128)(2,1)S(1)} %constant_dynamic-slice_fusion.2.x_ref.xall_ref) | copy-start | bytes 4718596
  82.8 48.3 %copy-start.4 = (bf16[4,2,192,768]{3,2,1,0:T(8,128)(2,1)}, bf16[4,2,192,768]{3,2,1,0:T(8,128)(2,1)S(1)}, u32[]{:S(2)}) copy-start(bf16[4,2,192,768]{3,2,1,0:T(8,128)(2,1)S(1)} %get-tuple-element.142) | copy-start | bytes 7077892
  84.4 5.3 %copy-start.21 = (bf16[4,1,192,768]{3,2,1,0:T(8,128)(2,1)}, bf16[4,1,192,768]{3,2,1,0:T(8,128)(2,1)S(1)}, u32[]{:S(2)}) copy-start(bf16[4,1,192,768]{3,2,1,0:T(8,128)(2,1)S(1)} %get-tuple-element.179) | copy-start | bytes 3538948
  127.6 4.1 copy-start.10
  127.6 4.1 copy-start.38
  147.7 4.8 %copy-start.18 = (bf16[1024,768]{1,0:T(8,128)(2,1)S(1)}, bf16[1024,768]{1,0:T(8,128)(2,1)}, u32[]{:S(2)}) copy-start(bf16[1024,768]{1,0:T(8,128)(2,1)} %fusion.46) | copy-start | bytes 4718596
  152.5 14.6 %copy-start.11 = (bf16[1,1,8,96,768]{4,3,0,1,2:T(8,128)(2,1)}, bf16[1,1,8,96,768]{4,3,0,1,2:T(8,128)(2,1)S(1)}, u32[]{:S(2)}) copy-start(bf16[1,1,8,96,768]{4,3,0,1,2:T(8,128)(2,1)S(1)} %get-tuple-element.136) | copy-start | bytes 3538948
  152.5 18.5 %copy-start.24 = (bf16[1,1,8,96,768]{4,3,0,1,2:T(8,128)(2,1)}, bf16[1,1,8,96,768]{4,3,0,1,2:T(8,128)(2,1)S(1)}, u32[]{:S(2)}) copy-start(bf16[1,1,8,96,768]{4,3,0,1,2:T(8,128)(2,1)S(1)} %get-tuple-element.135) | copy-start | bytes 3538948
  156.4 16.3 %copy-start.48 = (bf16[1024,768]{0,1:T(8,128)(2,1)}, bf16[1024,768]{0,1:T(8,128)(2,1)S(1)}, u32[]{:S(2)}) copy-start(bf16[1024,768]{0,1:T(8,128)(2,1)S(1)} %get-tuple-element.175) | copy-start | bytes 4718596
  191.8 5.3 %copy-start.47 = (f32[1024,768]{0,1:T(8,128)S(1)}, f32[1024,768]{0,1:T(8,128)}, u32[]{:S(2)}) copy-start(f32[1024,768]{0,1:T(8,128)} %get-tuple-element.172) | copy-start | bytes 9437188
  197.1 20.0 %copy-start.8 = (bf16[1024,768]{0,1:T(8,128)(2,1)}, bf16[1024,768]{0,1:T(8,128)(2,1)S(1)}, u32[]{:S(2)}) copy-start(bf16[1024,768]{0,1:T(8,128)(2,1)S(1)} %fusion.44) | copy-start | bytes 4718596
  217.3 5.4 %copy-start.7 = (bf16[1024,3072]{0,1:T(8,128)(2,1)}, bf16[1024,3072]{0,1:T(8,128)(2,1)S(1)}, u32[]{:S(2)}) copy-start(bf16[1024,3072]{0,1:T(8,128)(2,1)S(1)} %constant_dynamic-update-slice_fusion) | copy-start | bytes 18874372
  240.8 133.7 %reduce-scatter.6.cloned.1.call-start = ((), (), s32[]{:S(2)}) async-start(), calls=%async_computation.5 | async-start | bytes 5308416 | tf_op jit(solution)/shard_map/reduce_scatter | solution.py:217
  240.8 3.7 copy-start.3
  320.4 95.5 %reduce-scatter.8.cloned.1.call-start = ((), (), s32[]{:S(2)}) async-start(), calls=%async_computation.6 | async-start | bytes 2211840 | tf_op jit(solution)/shard_map/reduce_scatter | solution.py:235
  320.5 4.8 %copy-start.32 = (f32[768]{0:T(1024)S(1)}, f32[768]{0:T(1024)}, u32[]{:S(2)}) copy-start(f32[768]{0:T(1024)} %get-tuple-element.132) | copy-start | bytes 9220
  320.5 4.8 %copy-start.36 = (f32[768]{0:T(1024)S(1)}, f32[768]{0:T(1024)}, u32[]{:S(2)}) copy-start(f32[768]{0:T(1024)} %get-tuple-element.118) | copy-start | bytes 9220
  320.5 4.8 %copy-start.35 = (f32[768]{0:T(1024)S(1)}, f32[768]{0:T(1024)}, u32[]{:S(2)}) copy-start(f32[768]{0:T(1024)} %get-tuple-element.123) | copy-start | bytes 9220
  320.5 4.8 %copy-start.30 = (f32[768]{0:T(1024)S(1)}, f32[768]{0:T(1024)}, u32[]{:S(2)}) copy-start(f32[768]{0:T(1024)} %get-tuple-element.130) | copy-start | bytes 9220
  320.5 4.8 %copy-start.34 = (f32[768]{0:T(1024)S(1)}, f32[768]{0:T(1024)}, u32[]{:S(2)}) copy-start(f32[768]{0:T(1024)} %get-tuple-element.116) | copy-start | bytes 9220
  320.5 4.9 %copy-start.33 = (f32[768]{0:T(1024)S(1)}, f32[768]{0:T(1024)}, u32[]{:S(2)}) copy-start(f32[768]{0:T(1024)} %get-tuple-element.121) | copy-start | bytes 9220
  320.5 45.0 %copy-start.27 = (bf16[96,6144]{1,0:T(8,128)(2,1)S(1)}, bf16[96,6144]{1,0:T(8,128)(2,1)}, u32[]{:S(2)}) copy-start(bf16[96,6144]{1,0:T(8,128)(2,1)} %reduce-scatter.4.cloned.1.call-done) | copy-start | bytes 3538948
  320.5 45.1 %copy-start.22 = (bf16[4,1,192,768]{3,2,1,0:T(8,128)(2,1)S(1)}, bf16[4,1,192,768]{3,2,1,0:T(8,128)(2,1)}, u32[]{:S(2)}) copy-start(bf16[4,1,192,768]{3,2,1,0:T(8,128)(2,1)} %copy-done.21) | copy-start | bytes 3538948
  375.6 44.6 %copy-start.1 = (s32[4,1024]{1,0:T(4,128)S(1)}, s32[4,1024]{1,0:T(4,128)}, u32[]{:S(2)}) copy-start(s32[4,1024]{1,0:T(4,128)} %param.19) | copy-start | bytes 49156
  (28 other events, 64.8 us)
Sparse Core Ops, SparseCore 0:
  10.2 53.1 all-gather.5
  66.8 80.8 all-gather.7
  240.9 75.0 reduce-scatter.3
  320.5 52.7 reduce-scatter.5
  377.1 38.7 reduce-scatter.7
